TPU v7x, 512 devices: a whole 4x8x8 slice. The times are simulated.
512 devices in a mesh: leaf: 16 (over y, core), sub: 32 (over x, z).
Axes of the slice: x: 4, y: 8, z: 8, core: 2. Of those that a mesh axis runs over, the one named last changes fastest.
Arguments:
- panels: bfloat16 [3072, 4, 256, 128], P(('leaf', 'sub')), may hold values from -1 to 1
- root_panels: bfloat16 [3072, 256, 128], P(('leaf', 'sub')), may hold values from -1 to 1
- low_inverse: bfloat16 [3072, 128, 128], P(('leaf', 'sub')), may hold values from -4 to 1.5, as said below
- structure: int32 [3072, 4], P(('leaf', 'sub')), may hold values from 0 to 31, all different within a row; in each aligned block of 6 rows (0 to 5, 6 to 11, ...) at most 2 rows name the same one
- owner_map: int32 [16, 32], replicated, may hold values from 0 to 31, each once within a row
- upper_block: float32 [512, 256, 256], P(('leaf', 'sub')), may hold values from -1 to 10, as said below
- upper_cot: float32 [512, 256, 256], P(('leaf', 'sub')), may hold values from -6 to 6
- root_block: float32 [256, 256], replicated, may hold values from -1 to 10, as said below
- root_cot: float32 [256, 256], replicated, may hold values from -6 to 6
Outputs:
- panel_grad: bfloat16 [3072, 4, 256, 128], P(('leaf', 'sub'))
- root_grad: bfloat16 [3072, 256, 128], P(('leaf', 'sub'))
Inputs may be any that keep to these rules, and one draw needn't show every extreme that they name: `structure`: among the 6 rows of one device no upper supernode is named more than 2 times; the names within a row differ. Each row of owner_map is a permutation of the group's devices. `upper_block`: Symmetric; diagonal from 6 to 10, every off-diagonal entry at most 2 / 256 in size, so that the diagonal dominates its row. `root_block`: Symmetric; diagonal from 8 to 10, every off-diagonal entry at most 1 / 256 in size, so that the diagonal dominates its row. `low_inverse`: lower triangular, diagonal from 0.5 to 1.5.
All inputs are finite; a program needn't handle non-finite values.
Results may differ from a plain program's by a relative error of at most 0.0014.
The roundings to bfloat16 on the way count: a program that leaves them out, or rounds other values in their place, can miss the bound.
Values may be sent and summed in bfloat16 or wider, within the bound.
A program may use at most 64 MiB of HBM per device.

v0:
```python
import jax
import jax.numpy as jnp
from jax import lax
from jax.experimental import pallas as pl
from jax.experimental.pallas import tpu as pltpu
from jax.sharding import PartitionSpec as P

MESH = pl.DeviceIdType.MESH

def _allreduce_kernel(
    x_ref, o_ref, full, a1, a2, a3, rs1, rs2, rs3, rs4, ssem, rsem1, rsem2, rsem3, rsem4, gsem3, gsem2, gsem1
):
    leaf = lax.axis_index("leaf")
    sub = lax.axis_index("sub")
    c = leaf % 2
    y = leaf // 2
    x = sub // 8
    z = sub % 8

    def core_peer():
        return (leaf + 1 - 2 * c, sub)

    def x_peer(xx):
        return (leaf, xx * 8 + z)

    def y_peer(yy):
        return (yy * 2 + c, sub)

    def z_peer(zz):
        return (leaf, x * 8 + zz)

    peers = [core_peer()]
    peers += [x_peer((x + d) % 4) for d in range(1, 4)]
    peers += [y_peer((y + d) % 8) for d in range(1, 8)]
    peers += [z_peer((z + d) % 8) for d in range(1, 8)]
    barrier = pltpu.get_barrier_semaphore()
    for p in peers:
        pl.semaphore_signal(barrier, inc=1, device_id=p, device_id_type=MESH)
    pl.semaphore_wait(barrier, len(peers))

    sends = []

    def send(src, dst, rsem, dev):
        cp = pltpu.make_async_remote_copy(
            src_ref=src, dst_ref=dst, send_sem=ssem.at[len(sends)], recv_sem=rsem, device_id=dev, device_id_type=MESH
        )
        cp.start()
        sends.append(cp)

    def recv_wait(dst, rsem, dev):
        pltpu.make_async_remote_copy(
            src_ref=dst, dst_ref=dst, send_sem=ssem.at[0], recv_sem=rsem, device_id=dev, device_id_type=MESH
        ).wait_recv()

    mine1 = pl.multiple_of(c * 256, 256)
    send(x_ref.at[pl.ds(pl.multiple_of((1 - c) * 256, 256), 256)], rs1, rsem1.at[0], core_peer())
    recv_wait(rs1, rsem1.at[0], core_peer())
    a1[...] = x_ref[pl.ds(mine1, 256), :] + rs1[...]

    for d in range(1, 4):
        xx = (x + d) % 4
        send(a1.at[pl.ds(pl.multiple_of(xx * 64, 64), 64)], rs2.at[x], rsem2.at[x], x_peer(xx))
    for d in range(1, 4):
        xx = (x + d) % 4
        recv_wait(rs2.at[xx], rsem2.at[xx], x_peer(xx))
    rs2[x] = a1[pl.ds(pl.multiple_of(x * 64, 64), 64), :]
    a2[...] = rs2[0] + rs2[1] + rs2[2] + rs2[3]

    for d in range(1, 8):
        yy = (y + d) % 8
        send(a2.at[pl.ds(pl.multiple_of(yy * 8, 8), 8)], rs3.at[y], rsem3.at[y], y_peer(yy))
    for d in range(1, 8):
        yy = (y + d) % 8
        recv_wait(rs3.at[yy], rsem3.at[yy], y_peer(yy))
    rs3[y] = a2[pl.ds(pl.multiple_of(y * 8, 8), 8), :]
    total3 = rs3[0]
    for i in range(1, 8):
        total3 = total3 + rs3[i]
    a3[...] = total3

    for d in range(1, 8):
        zz = (z + d) % 8
        send(a3, rs4.at[z], rsem4.at[z], z_peer(zz))
    for d in range(1, 8):
        zz = (z + d) % 8
        recv_wait(rs4.at[zz], rsem4.at[zz], z_peer(zz))
    rs4[z] = a3[...]
    total4 = rs4[0]
    for i in range(1, 8):
        total4 = total4 + rs4[i]
    base2 = c * 256 + x * 64
    full[pl.ds(pl.multiple_of(base2 + y * 8, 8), 8), :] = total4

    for d in range(1, 8):
        yy = (y + d) % 8
        blk = full.at[pl.ds(pl.multiple_of(base2 + y * 8, 8), 8)]
        send(blk, blk, gsem3.at[y], y_peer(yy))
    for d in range(1, 8):
        yy = (y + d) % 8
        recv_wait(full.at[pl.ds(pl.multiple_of(base2 + yy * 8, 8), 8)], gsem3.at[yy], y_peer(yy))
    for d in range(1, 4):
        xx = (x + d) % 4
        blk = full.at[pl.ds(pl.multiple_of(base2, 64), 64)]
        send(blk, blk, gsem2.at[x], x_peer(xx))
    for d in range(1, 4):
        xx = (x + d) % 4
        recv_wait(full.at[pl.ds(pl.multiple_of(c * 256 + xx * 64, 64), 64)], gsem2.at[xx], x_peer(xx))
    blk = full.at[pl.ds(mine1, 256)]
    send(blk, blk, gsem1.at[0], core_peer())
    recv_wait(full.at[pl.ds(pl.multiple_of((1 - c) * 256, 256), 256)], gsem1.at[0], core_peer())
    for cp in sends:
        cp.wait_send()
    o_ref[...] = full[...]


def allreduce_root(gram):
    flat = gram.reshape(512, 128)
    n_sends = 1 + 3 + 7 + 7 + 7 + 3 + 1
    out = pl.pallas_call(
        _allreduce_kernel,
        out_shape=jax.ShapeDtypeStruct((512, 128), jnp.float32),
        in_specs=[pl.BlockSpec(memory_space=pltpu.VMEM)],
        out_specs=pl.BlockSpec(memory_space=pltpu.VMEM),
        scratch_shapes=[
            pltpu.VMEM((512, 128), jnp.float32),
            pltpu.VMEM((256, 128), jnp.float32),
            pltpu.VMEM((64, 128), jnp.float32),
            pltpu.VMEM((8, 128), jnp.float32),
            pltpu.VMEM((256, 128), jnp.float32),
            pltpu.VMEM((4, 64, 128), jnp.float32),
            pltpu.VMEM((8, 8, 128), jnp.float32),
            pltpu.VMEM((8, 8, 128), jnp.float32),
            pltpu.SemaphoreType.DMA((n_sends,)),
            pltpu.SemaphoreType.DMA((1,)),
            pltpu.SemaphoreType.DMA((4,)),
            pltpu.SemaphoreType.DMA((8,)),
            pltpu.SemaphoreType.DMA((8,)),
            pltpu.SemaphoreType.DMA((8,)),
            pltpu.SemaphoreType.DMA((4,)),
            pltpu.SemaphoreType.DMA((1,)),
        ],
        compiler_params=pltpu.CompilerParams(collective_id=0, has_side_effects=True),
        cost_estimate=pl.CostEstimate(flops=4 * 65536, bytes_accessed=3 * 262144, transcendentals=0),
    )(flat)
    return out.reshape(256, 256)


def adjoint_block(schur, cotangent):
    factor = jnp.linalg.cholesky(schur)
    identity = jnp.eye(schur.shape[0], dtype=schur.dtype)
    inverse = jax.scipy.linalg.solve_triangular(factor, identity, lower=True)
    product = jnp.dot(factor.T, cotangent, precision=lax.Precision.HIGHEST)
    lowered = jnp.tril(product) - 0.5 * jnp.diag(jnp.diag(product))
    adjoint_full = jnp.dot(
        jnp.dot(inverse.T, lowered, precision=lax.Precision.HIGHEST),
        inverse,
        precision=lax.Precision.HIGHEST,
    )
    return (0.5 * (adjoint_full + adjoint_full.T)).astype(jnp.bfloat16)


def body(
    panels,
    root_panels,
    low_inverse,
    structure,
    owner_map,
    upper_block,
    upper_cot,
    root_block,
    root_cot,
):
    devices_sub = lax.axis_size("sub")
    local_gram = jnp.einsum(
        "sbw,scw->bc", root_panels, root_panels, preferred_element_type=jnp.float32
    )
    root_total = allreduce_root(local_gram)
    root_total, panels = lax.optimization_barrier((root_total, panels))
    root_adjoint = adjoint_block(root_block - root_total, root_cot)
    rows_dev, blocks_row, height, breadth = panels.shape
    item_count = rows_dev * blocks_row
    capacity = max(2, 2 * item_count // devices_sub)
    group_id = lax.axis_index("leaf")
    owners = lax.dynamic_index_in_dim(owner_map, group_id, 0, keepdims=False)
    target = jnp.take(owners, structure.reshape(item_count))
    onehot = (target[:, None] == jnp.arange(devices_sub, dtype=jnp.int32)[None, :]).astype(
        jnp.int32
    )
    earlier = jnp.cumsum(onehot, axis=0) - onehot
    slot_id = jnp.sum(earlier * onehot, axis=1)
    position = target * capacity + slot_id
    flat_panels = panels.reshape(item_count, height, breadth)
    outgoing = (
        jnp.zeros((devices_sub * capacity, height, breadth), jnp.bfloat16)
        .at[position]
        .set(flat_panels)
    )
    incoming = lax.all_to_all(outgoing, "sub", split_axis=0, concat_axis=0, tiled=True)
    root_adjoint, incoming = lax.optimization_barrier((root_adjoint, incoming))
    gram_sum = jnp.einsum("nbw,ncw->bc", incoming, incoming, preferred_element_type=jnp.float32)
    upper_adjoint = adjoint_block(upper_block[0] - gram_sum, upper_cot[0])
    answer = (
        -2.0
        * jnp.einsum("bc,ncw->nbw", upper_adjoint, incoming, preferred_element_type=jnp.float32)
    ).astype(jnp.bfloat16)
    returned = lax.all_to_all(answer, "sub", split_axis=0, concat_axis=0, tiled=True)
    panel_adjoint = returned[position]
    panel_adjoint = panel_adjoint.reshape(rows_dev, blocks_row, height, breadth)
    panel_grad = jnp.einsum(
        "srbw,swv->srbv", panel_adjoint, low_inverse, preferred_element_type=jnp.float32
    ).astype(jnp.bfloat16)
    root_panel_adjoint = (
        -2.0
        * jnp.einsum("bc,scw->sbw", root_adjoint, root_panels, preferred_element_type=jnp.float32)
    ).astype(jnp.bfloat16)
    root_grad = jnp.einsum(
        "sbw,swv->sbv", root_panel_adjoint, low_inverse, preferred_element_type=jnp.float32
    ).astype(jnp.bfloat16)
    return (panel_grad, root_grad)


def solution(mesh):
    in_specs = (
        P(("leaf", "sub"), None, None, None),
        P(("leaf", "sub"), None, None),
        P(("leaf", "sub"), None, None),
        P(("leaf", "sub"), None),
        P(),
        P(("leaf", "sub"), None, None),
        P(("leaf", "sub"), None, None),
        P(),
        P(),
    )
    out_specs = (P(("leaf", "sub"), None, None, None), P(("leaf", "sub"), None, None))
    return jax.shard_map(body, mesh=mesh, in_specs=in_specs, out_specs=out_specs, check_vma=False)
```

profile of v0, /device:TPU:8, one launch (start us, length us, event | category | flops | bytes accessed | tf_op | source)
XLA Modules:
  0.0 340.9 jit_solution(17723669613034597706)
XLA Ops:
  0.7 1.0 copy-done
  1.9 0.7 reshape.126.x_ref
  2.7 0.8 copy.28
  3.6 38.6 %shard_map.104 = f32[512,128]{1,0:T(8,128)} custom-call(f32[512,128]{1,0:T(8,128)} %reshape.126.x_ref), custom_call_target="tpu_custom_call" | custom-call | flops 262144 | bytes 786432 | tf_op jit(solution)/shard_map/pallas_call | solution.py:119
  42.1 1.0 reshape.127
  43.2 0.7 fusion.66
  43.9 0.7 gather_fusion.1
  44.9 3.0 broadcast_in_dim.48
  47.9 5.5 %scatter_fusion = bf16[64,256,128]{2,1,0:T(8,128)(2,1)} fusion(bf16[64,256,128]{2,1,0:T(8,128)(2,1)} %broadcast_in_dim.48, s32[24]{0:T(128)S(1)} %fusion.67, bf16[24,256,128]{2,1,0:T(8,128)(2,1)S(1)} %bitcast.137), kind=kCustom, calls=%fused_computation.4 | custom fusion | bytes 4718688 | tf_op jit(solution)/shard_map/scatter | solution.py:196
  53.5 7.1 %all-to-all-start = ((bf16[64,256,128]{2,1,0:T(8,128)(2,1)}), bf16[64,256,128]{2,1,0:T(8,128)(2,1)}, u32[]{:S(2)}, u32[]{:S(2)}) async-start(bf16[64,256,128]{2,1,0:T(8,128)(2,1)} %scatter_fusion), calls=%async_computation | async-start | bytes 8388608 | tf_op jit(solution)/shard_map/all_to_all | solution.py:198
  61.1 11.7 %cholesky.130 = f32[128,128]{1,0:T(8,128)S(1)} custom-call(f32[128,128]{1,0:T(8,128)S(1)} %cholesky.194), custom_call_target="Cholesky" | custom-call | tf_op jit(solution)/shard_map/jit(cholesky)/cholesky | solution.py:149
  72.9 9.8 %custom-call.17 = f32[1,128,128]{1,2,0:T(8,128)S(1)} custom-call(f32[1,128,128]{2,1,0:T(8,128)S(1)} %get-tuple-element.55), custom_call_target="InvertDiagBlocksLowerTriangular" | custom-call | tf_op jit(solution)/shard_map/jit(cholesky)/cholesky | solution.py:149
  83.2 11.7 %cholesky.147 = f32[128,128]{1,0:T(8,128)S(1)} custom-call(f32[128,128]{1,0:T(8,128)S(1)} %convolution_subtract_fusion.3), custom_call_target="Cholesky" | custom-call | tf_op jit(solution)/shard_map/jit(cholesky)/cholesky | solution.py:149
  95.0 0.7 compare_reduce_fusion.2
  96.9 3.7 %while.4 = (s32[]{:T(128)}, f32[256,256]{1,0:T(8,128)S(1)}, s32[2,2]{1,0:T(2,128)S(1)}, f32[2,128,128]{2,1,0:T(8,128)S(1)}, s32[]{:T(128)}) while((s32[]{:T(128)}, f32[256,256]{1,0:T(8,128)S(1)}, s32[2,2]{1,0:T(2,128)S(1)}, f32[2,128,128]{2,1,0:T(8,128)S(1)}, s32[]{:T(128)}) %tuple.51), condition=%wide.while_cond, body=%wide.while_body.sunk | while | flops 2 | bytes 131181 | solution.py:151
  97.0 0.6 fusion.106
  97.5 1.3 bitcast_dynamic-update-slice_fusion.4
  98.8 0.6 fusion.106
  99.4 1.3 bitcast_dynamic-update-slice_fusion.4
  100.7 30.4 %custom-call.18 = f32[2,128,128]{1,2,0:T(8,128)S(1)} custom-call(f32[2,128,128]{2,1,0:T(8,128)S(1)} %get-tuple-element.26), custom_call_target="InvertDiagBlocksLowerTriangular" | custom-call | tf_op jit(solution)/shard_map/jit(_solve_triangular)/triangular_solve | solution.py:151
  131.1 0.5 fusion.29
  131.6 2.3 gather_fusion
  134.9 0.7 fusion.19
  135.6 0.4 fusion.32
  136.3 19.5 %all-to-all-done = bf16[64,256,128]{2,1,0:T(8,128)(2,1)} async-done(((bf16[64,256,128]{2,1,0:T(8,128)(2,1)}), bf16[64,256,128]{2,1,0:T(8,128)(2,1)}, u32[]{:S(2)}, u32[]{:S(2)}) %all-to-all-start) | async-done | bytes 4194336 | tf_op jit(solution)/shard_map/all_to_all | solution.py:198
  155.8 4.7 %fusion.3 = f32[256,256]{0,1:T(8,128)S(1)} fusion(bf16[64,256,128]{2,1,0:T(8,128)(2,1)} %all-to-all-done, f32[1,256,256]{1,2,0:T(8,128)S(1)} %copy.30), kind=kOutput, calls=%fused_computation.18 | convolution fusion | flops 1073807360 | bytes 4718592 | tf_op jit(solution)/shard_map/nbw,ncw->bc/dot_general | solution.py:200
  160.8 11.7 %cholesky.164 = f32[128,128]{1,0:T(8,128)S(1)} custom-call(f32[128,128]{1,0:T(8,128)S(1)} %cholesky.197), custom_call_target="Cholesky" | custom-call | tf_op jit(solution)/shard_map/jit(cholesky)/cholesky | solution.py:149
  172.5 9.8 %custom-call.19 = f32[1,128,128]{1,2,0:T(8,128)S(1)} custom-call(f32[1,128,128]{2,1,0:T(8,128)S(1)} %get-tuple-element.51), custom_call_target="InvertDiagBlocksLowerTriangular" | custom-call | tf_op jit(solution)/shard_map/jit(cholesky)/cholesky | solution.py:149
  182.8 11.9 %cholesky.181 = f32[128,128]{1,0:T(8,128)S(1)} custom-call(f32[128,128]{1,0:T(8,128)S(1)} %convolution_subtract_fusion.2), custom_call_target="Cholesky" | custom-call | tf_op jit(solution)/shard_map/jit(cholesky)/cholesky | solution.py:149
  194.8 0.6 compare_reduce_fusion
  195.4 0.6 compare_reduce_fusion.1
  197.4 3.9 %while.5 = (s32[]{:T(128)}, f32[256,256]{1,0:T(8,128)S(1)}, s32[2,2]{1,0:T(2,128)S(1)}, f32[2,128,128]{2,1,0:T(8,128)S(1)}, s32[]{:T(128)}) while((s32[]{:T(128)}, f32[256,256]{1,0:T(8,128)S(1)}, s32[2,2]{1,0:T(2,128)S(1)}, f32[2,128,128]{2,1,0:T(8,128)S(1)}, s32[]{:T(128)}) %tuple.57), condition=%wide.while_cond.clone, body=%wide.while_body.clone.sunk | while | flops 2 | bytes 131181 | solution.py:151
  197.4 0.6 fusion.107
  198.0 1.4 bitcast_dynamic-update-slice_fusion.5
  199.4 0.6 fusion.107
  199.9 1.4 bitcast_dynamic-update-slice_fusion.5
  201.3 19.7 %custom-call.20 = f32[2,128,128]{1,2,0:T(8,128)S(1)} custom-call(f32[2,128,128]{2,1,0:T(8,128)S(1)} %get-tuple-element.27), custom_call_target="InvertDiagBlocksLowerTriangular" | custom-call | tf_op jit(solution)/shard_map/jit(_solve_triangular)/triangular_solve | solution.py:151
  221.0 0.3 fusion.51
  221.9 0.5 fusion.7
  222.4 2.3 gather_fusion.2
  224.8 0.7 fusion.22
  225.4 0.4 fusion.31
  226.0 5.5 %fusion = bf16[64,256,128]{1,2,0:T(8,128)(2,1)} fusion(bf16[64,256,128]{2,1,0:T(8,128)(2,1)} %all-to-all-done, f32[256,256]{1,0:T(8,128)S(1)} %fusion.31, f32[256,256]{0,1:T(8,128)S(1)} %copy.33), kind=kOutput, calls=%fused_computation.10 | convolution fusion | flops 1078132736 | bytes 8912896 | tf_op jit(solution)/shard_map/bc,ncw->nbw/dot_general | solution.py:204
  231.4 7.3 %all-to-all-start.1 = ((bf16[64,256,128]{1,2,0:T(8,128)(2,1)}), bf16[64,256,128]{1,2,0:T(8,128)(2,1)}, u32[]{:S(2)}, u32[]{:S(2)}) async-start(bf16[64,256,128]{1,2,0:T(8,128)(2,1)} %fusion), calls=%async_computation.1 | async-start | bytes 8388608 | tf_op jit(solution)/shard_map/all_to_all | solution.py:206
  238.8 1.2 convolution_convert_fusion.1
  240.0 96.0 %all-to-all-done.1 = bf16[64,256,128]{1,2,0:T(8,128)(2,1)} async-done(((bf16[64,256,128]{1,2,0:T(8,128)(2,1)}), bf16[64,256,128]{1,2,0:T(8,128)(2,1)}, u32[]{:S(2)}, u32[]{:S(2)}) %all-to-all-start.1) | async-done | bytes 4194336 | tf_op jit(solution)/shard_map/all_to_all | solution.py:206
  336.0 2.8 gather_fusion.3
  338.8 1.8 convolution_convert_fusion
  (64 shorter events, 4.7 us)
Async XLA Ops:
  0.6 1.0 copy-start
  0.6 47.3 %copy-start.1 = (bf16[6,4,256,128]{3,2,1,0:T(8,128)(2,1)S(1)}, bf16[6,4,256,128]{3,2,1,0:T(8,128)(2,1)}, u32[]{:S(2)}) copy-start(bf16[6,4,256,128]{3,2,1,0:T(8,128)(2,1)} %param.12) | copy-start | bytes 4718596
  53.5 7.3 %copy-start.3 = (f32[256,256]{1,0:T(8,128)S(1)}, f32[256,256]{1,0:T(8,128)}, u32[]{:S(2)}) copy-start(f32[256,256]{1,0:T(8,128)} %param.19) | copy-start | bytes 786436
  53.5 102.3 %all-to-all-start = ((bf16[64,256,128]{2,1,0:T(8,128)(2,1)}), bf16[64,256,128]{2,1,0:T(8,128)(2,1)}, u32[]{:S(2)}, u32[]{:S(2)}) async-start(bf16[64,256,128]{2,1,0:T(8,128)(2,1)} %scatter_fusion), calls=%async_computation | async-start | bytes 8388608 | tf_op jit(solution)/shard_map/all_to_all | solution.py:198
  60.6 70.5 %copy-start.5 = (f32[256,256]{1,0:T(8,128)S(1)}, f32[256,256]{1,0:T(8,128)}, u32[]{:S(2)}) copy-start(f32[256,256]{1,0:T(8,128)} %param.20) | copy-start | bytes 786436
  61.1 75.0 %copy-start.4 = (f32[1,256,256]{2,1,0:T(8,128)S(1)}, f32[1,256,256]{2,1,0:T(8,128)}, u32[]{:S(2)}) copy-start(f32[1,256,256]{2,1,0:T(8,128)} %param.17) | copy-start | bytes 786436
  160.6 61.3 %copy-start.6 = (f32[1,256,256]{2,1,0:T(8,128)S(1)}, f32[1,256,256]{2,1,0:T(8,128)}, u32[]{:S(2)}) copy-start(f32[1,256,256]{2,1,0:T(8,128)} %param.18) | copy-start | bytes 786436
  231.4 7.3 %copy-start.2 = (bf16[6,128,128]{2,1,0:T(8,128)(2,1)S(1)}, bf16[6,128,128]{2,1,0:T(8,128)(2,1)}, u32[]{:S(2)}) copy-start(bf16[6,128,128]{2,1,0:T(8,128)(2,1)} %param.14) | copy-start | bytes 589828
  231.4 104.5 %all-to-all-start.1 = ((bf16[64,256,128]{1,2,0:T(8,128)(2,1)}), bf16[64,256,128]{1,2,0:T(8,128)(2,1)}, u32[]{:S(2)}, u32[]{:S(2)}) async-start(bf16[64,256,128]{1,2,0:T(8,128)(2,1)} %fusion), calls=%async_computation.1 | async-start | bytes 8388608 | tf_op jit(solution)/shard_map/all_to_all | solution.py:206
where the time goes:
time: 344 us; the launch traced here: 341 us
  other arithmetic  119 us (35%)
  waiting for transfers between devices  115 us (33%)
  Pallas kernels  38.6 us (11%)
  local copies, waits for them, and re-layouts  29.8 us (9%)
  matrix products  19.3 us (6%)
  starting transfers between devices  14.4 us (4%)
  between operations  3.85 us (1%)
    all_to_all x1, waiting for transfers between devices, body(): lax.all_to_all(answer, 'sub', split_axis=0, concat_axis=0, tiled=True)  96 us
    another operation x13, other arithmetic, adjoint_block(): factor = jnp.linalg.cholesky(schur)  68.7 us
    another operation x5, other arithmetic, adjoint_block(): inverse = jax.scipy.linalg.solve_triangular(factor, identity, lower=True)  50.1 us
    pallas_call x1, Pallas kernels, allreduce_root(): pl.pallas_call(_allreduce_kernel, out_shape=jax.ShapeDtypeStruct((512, 12...  38.6 us
    all_to_all x1, waiting for transfers between devices, body(): lax.all_to_all(outgoing, 'sub', split_axis=0, concat_axis=0, tiled=True)  19.5 us
    another operation x15, local copies, waits for them, and re-layouts, adjoint_block(): inverse = jax.scipy.linalg.solve_triangular(factor, identity, lower=True)  7.68 us
    all_to_all x1, starting transfers between devices, body(): lax.all_to_all(answer, 'sub', split_axis=0, concat_axis=0, tiled=True)  7.29 us
    all_to_all x1, starting transfers between devices, body(): lax.all_to_all(outgoing, 'sub', split_axis=0, concat_axis=0, tiled=True)  7.1 us
  transfers between devices with their start and end apart: 2, of which 2 were waited for; matrix products, arithmetic and copies ran while one was open for 22% of the time, Pallas kernels for 0%

commit v1 on v0

--- a/solution.py
+++ b/solution.py
@@ -145,6 +145,98 @@
     return out.reshape(256, 256)
 
 
+def _gather_kernel(a_ref, o_ref, gathered, ssem, rsz, rsx, lsem):
+    leaf = lax.axis_index("leaf")
+    sub = lax.axis_index("sub")
+    x = sub // 8
+    z = sub % 8
+    peers = [(leaf, x * 8 + (z + d) % 8) for d in range(1, 8)]
+    peers += [(leaf, ((x + d) % 4) * 8 + z) for d in range(1, 4)]
+    barrier = pltpu.get_barrier_semaphore()
+    for p in peers:
+        pl.semaphore_signal(barrier, inc=1, device_id=p, device_id_type=MESH)
+    pl.semaphore_wait(barrier, len(peers))
+
+    sends = []
+
+    def send(src, dst, rsem, dev):
+        cp = pltpu.make_async_remote_copy(
+            src_ref=src, dst_ref=dst, send_sem=ssem.at[len(sends)], recv_sem=rsem, device_id=dev, device_id_type=MESH
+        )
+        cp.start()
+        sends.append(cp)
+
+    def recv_wait(dst, rsem, dev):
+        pltpu.make_async_remote_copy(
+            src_ref=dst, dst_ref=dst, send_sem=ssem.at[0], recv_sem=rsem, device_id=dev, device_id_type=MESH
+        ).wait_recv()
+
+    for d in range(1, 8):
+        zz = (z + d) % 8
+        send(a_ref, gathered.at[x * 8 + z], rsz.at[z], (leaf, x * 8 + zz))
+    own = pltpu.make_async_copy(a_ref, gathered.at[x * 8 + z], lsem.at[0])
+    own.start()
+    for d in range(1, 8):
+        zz = (z + d) % 8
+        recv_wait(gathered.at[x * 8 + zz], rsz.at[zz], (leaf, x * 8 + zz))
+    own.wait()
+    column = gathered.at[pl.ds(pl.multiple_of(x * 8, 8), 8)]
+    for d in range(1, 4):
+        xx = (x + d) % 4
+        send(column, column, rsx.at[x], (leaf, xx * 8 + z))
+    for d in range(1, 4):
+        xx = (x + d) % 4
+        recv_wait(gathered.at[pl.ds(pl.multiple_of(xx * 8, 8), 8)], rsx.at[xx], (leaf, xx * 8 + z))
+    for cp in sends:
+        cp.wait_send()
+    o_ref[...] = gathered[...]
+
+
+def gather_sub(block):
+    rows = block.shape[0]
+    return pl.pallas_call(
+        _gather_kernel,
+        out_shape=jax.ShapeDtypeStruct((32, rows, 128), block.dtype),
+        in_specs=[pl.BlockSpec(memory_space=pltpu.VMEM)],
+        out_specs=pl.BlockSpec(memory_space=pltpu.VMEM),
+        scratch_shapes=[
+            pltpu.VMEM((32, rows, 128), block.dtype),
+            pltpu.SemaphoreType.DMA((10,)),
+            pltpu.SemaphoreType.DMA((8,)),
+            pltpu.SemaphoreType.DMA((4,)),
+            pltpu.SemaphoreType.DMA((1,)),
+        ],
+        compiler_params=pltpu.CompilerParams(collective_id=1, has_side_effects=True),
+        cost_estimate=pl.CostEstimate(flops=0, bytes_accessed=2 * 32 * rows * 128 * 2, transcendentals=0),
+    )(block)
+
+
+def pack_symmetric(a):
+    h = a.shape[0] // 2
+    row = lax.broadcasted_iota(jnp.int32, (h, h), 0)
+    col = lax.broadcasted_iota(jnp.int32, (h, h), 1)
+    folded = jnp.where(col <= row, a[:h, :h], a[h:, h:])
+    diag = jnp.where(row == col, a[h:, h:], jnp.zeros_like(a[h:, h:]))
+    diag_row = jnp.sum(diag.astype(jnp.float32), axis=0, keepdims=True).astype(a.dtype)
+    pad = jnp.zeros((15, h), a.dtype)
+    return jnp.concatenate([folded, a[h:, :h], diag_row, pad], axis=0)
+
+
+def unpack_symmetric(packed):
+    h = 128
+    folded = packed[:, :h, :]
+    lower = packed[:, h:2 * h, :]
+    diag_row = packed[:, 2 * h:2 * h + 1, :]
+    row = lax.broadcasted_iota(jnp.int32, (1, h, h), 1)
+    col = lax.broadcasted_iota(jnp.int32, (1, h, h), 2)
+    folded_t = jnp.swapaxes(folded, 1, 2)
+    top_left = jnp.where(col <= row, folded, folded_t)
+    bottom_right = jnp.where(col > row, folded, jnp.where(col < row, folded_t, diag_row))
+    top = jnp.concatenate([top_left, jnp.swapaxes(lower, 1, 2)], axis=2)
+    bottom = jnp.concatenate([lower, bottom_right], axis=2)
+    return jnp.concatenate([top, bottom], axis=1)
+
+
 def adjoint_block(schur, cotangent):
     factor = jnp.linalg.cholesky(schur)
     identity = jnp.eye(schur.shape[0], dtype=schur.dtype)
@@ -199,12 +291,12 @@
     root_adjoint, incoming = lax.optimization_barrier((root_adjoint, incoming))
     gram_sum = jnp.einsum("nbw,ncw->bc", incoming, incoming, preferred_element_type=jnp.float32)
     upper_adjoint = adjoint_block(upper_block[0] - gram_sum, upper_cot[0])
-    answer = (
+    every_adjoint = unpack_symmetric(gather_sub(pack_symmetric(upper_adjoint)))
+    chosen = jnp.take(every_adjoint, target, axis=0)
+    panel_adjoint = (
         -2.0
-        * jnp.einsum("bc,ncw->nbw", upper_adjoint, incoming, preferred_element_type=jnp.float32)
+        * jnp.einsum("nbc,ncw->nbw", chosen, flat_panels, preferred_element_type=jnp.float32)
     ).astype(jnp.bfloat16)
-    returned = lax.all_to_all(answer, "sub", split_axis=0, concat_axis=0, tiled=True)
-    panel_adjoint = returned[position]
     panel_adjoint = panel_adjoint.reshape(rows_dev, blocks_row, height, breadth)
     panel_grad = jnp.einsum(
         "srbw,swv->srbv", panel_adjoint, low_inverse, preferred_element_type=jnp.float32

time: 344 us -> 300 us (0.87)
  waiting for transfers between devices: 115 us -> 18.8 us
  Pallas kernels: 38.6 us -> 85.6 us
  other arithmetic: 119 us -> 128 us
  local copies, waits for them, and re-layouts: 29.8 us -> 37.2 us
  starting transfers between devices: 14.4 us -> 7.11 us
    all_to_all x1 -> x0, waiting for transfers between devices: 96 us -> none  [body(): lax.all_to_all(answer, 'sub', split_axis=0, concat_axis=0, tiled=True)]
    pallas_call x0 -> x1, Pallas kernels: none -> 47 us  [gather_sub(): pl.pallas_call(_gather_kernel, out_shape=jax.ShapeDtypeStruct((32, rows,...]
    all_to_all x1 -> x0, starting transfers between devices: 7.29 us -> none  [body(): lax.all_to_all(answer, 'sub', split_axis=0, concat_axis=0, tiled=True)]
    slice x0 -> x4, local copies, waits for them, and re-layouts: none -> 7.21 us  [the longest x2 4.75 us: unpack_symmetric(): folded = packed[:, :h, :]]
    concatenate x0 -> x2, other arithmetic: none -> 4.33 us  [the longest x1 3.59 us: unpack_symmetric(): return jnp.concatenate([top, bottom], axis=1)]
  transfers between devices with their start and end apart: 2 -> 1, of which waited for: 2 -> 1; matrix products, arithmetic and copies ran while one was open for 22% -> 25% of each run, Pallas kernels for 0% -> 0%
where the time goes in v1:
time: 300 us; the launch traced here: 296 us
  other arithmetic  128 us (43%)
  Pallas kernels  85.6 us (29%)
  local copies, waits for them, and re-layouts  37.2 us (12%)
  waiting for transfers between devices  18.8 us (6%)
  matrix products  16.2 us (5%)
  starting transfers between devices  7.11 us (2%)
  between operations  3.9 us (1%)
    another operation x13, other arithmetic, adjoint_block(): factor = jnp.linalg.cholesky(schur)  68.8 us
    another operation x5, other arithmetic, adjoint_block(): inverse = jax.scipy.linalg.solve_triangular(factor, identity, lower=True)  50.1 us
    pallas_call x1, Pallas kernels, gather_sub(): pl.pallas_call(_gather_kernel, out_shape=jax.ShapeDtypeStruct((32, rows,...  47 us
    pallas_call x1, Pallas kernels, allreduce_root(): pl.pallas_call(_allreduce_kernel, out_shape=jax.ShapeDtypeStruct((512, 12...  38.6 us
    all_to_all x1, waiting for transfers between devices, body(): lax.all_to_all(outgoing, 'sub', split_axis=0, concat_axis=0, tiled=True)  18.8 us
    another operation x15, local copies, waits for them, and re-layouts, adjoint_block(): inverse = jax.scipy.linalg.solve_triangular(factor, identity, lower=True)  7.81 us
    all_to_all x1, starting transfers between devices, body(): lax.all_to_all(outgoing, 'sub', split_axis=0, concat_axis=0, tiled=True)  7.11 us
  transfers between devices with their start and end apart: 1, of which 1 were waited for; matrix products, arithmetic and copies ran while one was open for 25% of the time, Pallas kernels for 0%

profile of v1, /device:TPU:8, one launch (start us, length us, event | category | flops | bytes accessed | tf_op | source)
XLA Modules:
  0.0 296.5 jit_solution(47174331796056174)
XLA Ops:
  0.6 1.0 copy-done
  1.9 0.7 reshape.191.x_ref
  2.7 0.8 copy.22
  3.6 38.6 %shard_map.104 = f32[512,128]{1,0:T(8,128)} custom-call(f32[512,128]{1,0:T(8,128)} %reshape.191.x_ref), custom_call_target="tpu_custom_call" | custom-call | flops 262144 | bytes 786432 | tf_op jit(solution)/shard_map/pallas_call | solution.py:119
  42.2 1.0 reshape.192
  43.2 0.7 fusion.77
  43.9 0.7 gather_fusion
  45.0 3.0 %broadcast_in_dim.97 = bf16[64,256,128]{2,1,0:T(8,128)(2,1)} broadcast(bf16[]{:T(256)} %constant.130.clone.1), dimensions={} | broadcast | bytes 4194306 | tf_op jit(solution)/shard_map/broadcast_in_dim | solution.py:286
  48.0 5.4 %scatter_fusion = bf16[64,256,128]{2,1,0:T(8,128)(2,1)} fusion(bf16[64,256,128]{2,1,0:T(8,128)(2,1)} %broadcast_in_dim.97, s32[24]{0:T(128)S(1)} %fusion.78, bf16[24,256,128]{2,1,0:T(8,128)(2,1)S(1)} %bitcast.141), kind=kCustom, calls=%fused_computation.4 | custom fusion | bytes 4718688 | tf_op jit(solution)/shard_map/scatter | solution.py:288
  53.4 7.1 %all-to-all-start = ((bf16[64,256,128]{2,1,0:T(8,128)(2,1)}), bf16[64,256,128]{2,1,0:T(8,128)(2,1)}, u32[]{:S(2)}, u32[]{:S(2)}) async-start(bf16[64,256,128]{2,1,0:T(8,128)(2,1)} %scatter_fusion), calls=%async_computation | async-start | bytes 8388608 | tf_op jit(solution)/shard_map/all_to_all | solution.py:290
  61.0 11.7 %cholesky.130 = f32[128,128]{1,0:T(8,128)S(1)} custom-call(f32[128,128]{1,0:T(8,128)S(1)} %cholesky.194), custom_call_target="Cholesky" | custom-call | tf_op jit(solution)/shard_map/jit(cholesky)/cholesky | solution.py:241
  72.8 9.8 %custom-call.17 = f32[1,128,128]{1,2,0:T(8,128)S(1)} custom-call(f32[1,128,128]{2,1,0:T(8,128)S(1)} %get-tuple-element.65), custom_call_target="InvertDiagBlocksLowerTriangular" | custom-call | tf_op jit(solution)/shard_map/jit(cholesky)/cholesky | solution.py:241
  83.1 11.7 %cholesky.147 = f32[128,128]{1,0:T(8,128)S(1)} custom-call(f32[128,128]{1,0:T(8,128)S(1)} %convolution_subtract_fusion.3), custom_call_target="Cholesky" | custom-call | tf_op jit(solution)/shard_map/jit(cholesky)/cholesky | solution.py:241
  94.8 0.7 compare_reduce_fusion.2
  96.8 3.7 %while.4 = (s32[]{:T(128)}, f32[256,256]{1,0:T(8,128)S(1)}, s32[2,2]{1,0:T(2,128)S(1)}, f32[2,128,128]{2,1,0:T(8,128)S(1)}, s32[]{:T(128)}) while((s32[]{:T(128)}, f32[256,256]{1,0:T(8,128)S(1)}, s32[2,2]{1,0:T(2,128)S(1)}, f32[2,128,128]{2,1,0:T(8,128)S(1)}, s32[]{:T(128)}) %tuple.58), condition=%wide.while_cond, body=%wide.while_body.sunk | while | flops 2 | bytes 131181 | solution.py:243
  97.4 1.3 bitcast_dynamic-update-slice_fusion.4
  99.3 1.3 bitcast_dynamic-update-slice_fusion.4
  100.6 30.4 %custom-call.18 = f32[2,128,128]{1,2,0:T(8,128)S(1)} custom-call(f32[2,128,128]{2,1,0:T(8,128)S(1)} %get-tuple-element.26), custom_call_target="InvertDiagBlocksLowerTriangular" | custom-call | tf_op jit(solution)/shard_map/jit(_solve_triangular)/triangular_solve | solution.py:243
  131.5 2.3 gather_fusion.1
  134.8 0.7 fusion.26
  136.3 0.7 fusion.17
  137.0 18.8 %all-to-all-done = bf16[64,256,128]{2,1,0:T(8,128)(2,1)} async-done(((bf16[64,256,128]{2,1,0:T(8,128)(2,1)}), bf16[64,256,128]{2,1,0:T(8,128)(2,1)}, u32[]{:S(2)}, u32[]{:S(2)}) %all-to-all-start) | async-done | bytes 4194336 | tf_op jit(solution)/shard_map/all_to_all | solution.py:290
  155.8 4.7 %fusion.8 = f32[256,256]{0,1:T(8,128)S(1)} fusion(bf16[64,256,128]{2,1,0:T(8,128)(2,1)} %all-to-all-done, f32[1,256,256]{1,2,0:T(8,128)S(1)} %copy.24), kind=kOutput, calls=%fused_computation.22 | convolution fusion | flops 1073807360 | bytes 4718592 | tf_op jit(solution)/shard_map/nbw,ncw->bc/dot_general | solution.py:292
  160.8 11.7 %cholesky.164 = f32[128,128]{1,0:T(8,128)S(1)} custom-call(f32[128,128]{1,0:T(8,128)S(1)} %cholesky.197), custom_call_target="Cholesky" | custom-call | tf_op jit(solution)/shard_map/jit(cholesky)/cholesky | solution.py:241
  172.6 9.8 %custom-call.19 = f32[1,128,128]{1,2,0:T(8,128)S(1)} custom-call(f32[1,128,128]{2,1,0:T(8,128)S(1)} %get-tuple-element.61), custom_call_target="InvertDiagBlocksLowerTriangular" | custom-call | tf_op jit(solution)/shard_map/jit(cholesky)/cholesky | solution.py:241
  182.8 11.9 %cholesky.181 = f32[128,128]{1,0:T(8,128)S(1)} custom-call(f32[128,128]{1,0:T(8,128)S(1)} %convolution_subtract_fusion.2), custom_call_target="Cholesky" | custom-call | tf_op jit(solution)/shard_map/jit(cholesky)/cholesky | solution.py:241
  194.8 0.6 compare_reduce_fusion
  195.4 0.7 compare_reduce_fusion.1
  197.4 4.1 %while.5 = (s32[]{:T(128)}, f32[256,256]{1,0:T(8,128)S(1)}, s32[2,2]{1,0:T(2,128)S(1)}, f32[2,128,128]{2,1,0:T(8,128)S(1)}, s32[]{:T(128)}) while((s32[]{:T(128)}, f32[256,256]{1,0:T(8,128)S(1)}, s32[2,2]{1,0:T(2,128)S(1)}, f32[2,128,128]{2,1,0:T(8,128)S(1)}, s32[]{:T(128)}) %tuple.64), condition=%wide.while_cond.clone, body=%wide.while_body.clone.sunk | while | flops 2 | bytes 131181 | solution.py:243
  197.5 0.7 fusion.119
  198.1 1.3 bitcast_dynamic-update-slice_fusion.5
  199.5 0.7 fusion.119
  200.2 1.3 bitcast_dynamic-update-slice_fusion.5
  201.5 19.7 %custom-call.20 = f32[2,128,128]{1,2,0:T(8,128)S(1)} custom-call(f32[2,128,128]{2,1,0:T(8,128)S(1)} %get-tuple-element.27), custom_call_target="InvertDiagBlocksLowerTriangular" | custom-call | tf_op jit(solution)/shard_map/jit(_solve_triangular)/triangular_solve | solution.py:243
  222.6 2.3 gather_fusion.2
  225.0 0.7 fusion.29
  226.3 0.7 maximum_maximum_fusion.1.a_ref
  227.0 47.0 %shard_map.105 = bf16[32,272,128]{2,1,0:T(8,128)(2,1)} custom-call(bf16[272,128]{1,0:T(8,128)(2,1)} %maximum_maximum_fusion.1.a_ref), custom_call_target="tpu_custom_call" | custom-call | bytes 4456448 | tf_op jit(solution)/shard_map/pallas_call | solution.py:197
  274.0 2.5 slice.55
  276.5 0.8 slice.57
  277.3 2.3 copy.32
  279.6 3.0 %bitcast_select_fusion.1 = (bf16[32,128,128]{2,1,0:T(8,128)(2,1)}, bf16[32,128,128]{2,1,0:T(8,128)(2,1)}, bf16[32,128,128]{2,1,0:T(8,128)(2,1)}) fusion(bf16[32,128,128]{1,2,0:T(8,128)(2,1)} %copy.32, pred[128,128]{1,0:T(8,128)(4,1)S(1)} %iota_compare_fusion.8, bf16[32,272,128]{2,1,0:T(8,128)(2,1)S(1)} %copy-done.1, bf16[32,128]{1,0:T(8,128)(2,1)S(1)} %bitcast.143, ...), kind=kLoop, calls=%fused_computation.28 | loop fusion | flops 1572864 | bytes 6348800 | tf_op jit(solution)/shard_map/jit(_where)/select_n | solution.py:233
  282.6 1.6 copy.33
  284.3 3.6 %maximum_maximum_fusion = bf16[32,256,256]{2,1,0:T(8,128)(2,1)} fusion(bf16[32,128,128]{2,1,0:T(8,128)(2,1)} %get-tuple-element.53, bf16[32,128,128]{2,1,0:T(8,128)(2,1)} %get-tuple-element.54, bf16[32,128,128]{2,1,0:T(8,128)(2,1)S(1)} %bitcast.139, bf16[32,128,128]{2,1,0:T(8,128)(2,1)} %get-tuple-element.52), kind=kLoop, calls=%fused_computation.9 | loop fusion | flops 16777216 | bytes 8388608 | tf_op jit(solution)/shard_map/concatenate | solution.py:237
  287.9 2.9 gather_fusion.3
  290.8 2.5 multiply_convert_fusion
  293.3 1.7 convolution_convert_fusion
  295.0 1.2 convolution_convert_fusion.1
  (84 shorter events, 8.1 us)
Async XLA Ops:
  0.6 1.0 copy-start
  1.9 46.0 %copy-start.2 = (bf16[6,4,256,128]{3,2,1,0:T(8,128)(2,1)S(1)}, bf16[6,4,256,128]{3,2,1,0:T(8,128)(2,1)}, u32[]{:S(2)}) copy-start(bf16[6,4,256,128]{3,2,1,0:T(8,128)(2,1)} %param.12) | copy-start | bytes 4718596
  53.4 7.3 %copy-start.6 = (f32[256,256]{1,0:T(8,128)S(1)}, f32[256,256]{1,0:T(8,128)}, u32[]{:S(2)}) copy-start(f32[256,256]{1,0:T(8,128)} %param.19) | copy-start | bytes 786436
  53.4 102.4 %all-to-all-start = ((bf16[64,256,128]{2,1,0:T(8,128)(2,1)}), bf16[64,256,128]{2,1,0:T(8,128)(2,1)}, u32[]{:S(2)}, u32[]{:S(2)}) async-start(bf16[64,256,128]{2,1,0:T(8,128)(2,1)} %scatter_fusion), calls=%async_computation | async-start | bytes 8388608 | tf_op jit(solution)/shard_map/all_to_all | solution.py:290
  60.5 70.5 %copy-start.8 = (f32[256,256]{1,0:T(8,128)S(1)}, f32[256,256]{1,0:T(8,128)}, u32[]{:S(2)}) copy-start(f32[256,256]{1,0:T(8,128)} %param.20) | copy-start | bytes 786436
  96.8 39.2 %copy-start.7 = (f32[1,256,256]{2,1,0:T(8,128)S(1)}, f32[1,256,256]{2,1,0:T(8,128)}, u32[]{:S(2)}) copy-start(f32[1,256,256]{2,1,0:T(8,128)} %param.17) | copy-start | bytes 786436
  160.6 61.5 %copy-start.9 = (f32[1,256,256]{2,1,0:T(8,128)S(1)}, f32[1,256,256]{2,1,0:T(8,128)}, u32[]{:S(2)}) copy-start(f32[1,256,256]{2,1,0:T(8,128)} %param.18) | copy-start | bytes 786436
  274.0 5.6 %copy-start.1 = (bf16[32,272,128]{2,1,0:T(8,128)(2,1)S(1)}, bf16[32,272,128]{2,1,0:T(8,128)(2,1)}, u32[]{:S(2)}) copy-start(bf16[32,272,128]{2,1,0:T(8,128)(2,1)} %shard_map.105) | copy-start | bytes 6684676
  290.8 2.5 copy-start.3
  293.3 1.7 copy-start.4
  293.3 1.7 copy-start.5

commit v2 on v1

--- a/solution.py
+++ b/solution.py
@@ -237,10 +237,27 @@
     return jnp.concatenate([top, bottom], axis=1)
 
 
+def _dot(a, b):
+    return jnp.dot(a, b, precision=lax.Precision.HIGHEST)
+
+
+def factor_and_inverse(schur):
+    h = schur.shape[0] // 2
+    identity = jnp.eye(h, dtype=schur.dtype)
+    f11 = jnp.linalg.cholesky(schur[:h, :h])
+    i11 = jax.scipy.linalg.solve_triangular(f11, identity, lower=True)
+    f21 = _dot(schur[h:, :h], i11.T)
+    f22 = jnp.linalg.cholesky(schur[h:, h:] - _dot(f21, f21.T))
+    i22 = jax.scipy.linalg.solve_triangular(f22, identity, lower=True)
+    i21 = -_dot(_dot(i22, f21), i11)
+    zero = jnp.zeros((h, h), schur.dtype)
+    factor = jnp.concatenate([jnp.concatenate([f11, zero], 1), jnp.concatenate([f21, f22], 1)], 0)
+    inverse = jnp.concatenate([jnp.concatenate([i11, zero], 1), jnp.concatenate([i21, i22], 1)], 0)
+    return factor, inverse
+
+
 def adjoint_block(schur, cotangent):
-    factor = jnp.linalg.cholesky(schur)
-    identity = jnp.eye(schur.shape[0], dtype=schur.dtype)
-    inverse = jax.scipy.linalg.solve_triangular(factor, identity, lower=True)
+    factor, inverse = factor_and_inverse(schur)
     product = jnp.dot(factor.T, cotangent, precision=lax.Precision.HIGHEST)
     lowered = jnp.tril(product) - 0.5 * jnp.diag(jnp.diag(product))
     adjoint_full = jnp.dot(

time: 300 us -> 286 us (0.953)
  the two profiles are of different devices: /device:TPU:8 before, /device:TPU:64 now
where the time goes in v2:
time: 286 us; the launch traced here: 283 us
  other arithmetic  110 us (38%)
  Pallas kernels  85.1 us (30%)
  waiting for transfers between devices  32.7 us (11%)
  local copies, waits for them, and re-layouts  29.7 us (10%)
  matrix products  16.4 us (6%)
  starting transfers between devices  7.4 us (3%)
    pallas_call x1, Pallas kernels, gather_sub(): pl.pallas_call(_gather_kernel, out_shape=jax.ShapeDtypeStruct((32, rows,...  46.3 us
    pallas_call x1, Pallas kernels, allreduce_root(): pl.pallas_call(_allreduce_kernel, out_shape=jax.ShapeDtypeStruct((512, 12...  38.8 us
    all_to_all x1, waiting for transfers between devices, body(): lax.all_to_all(outgoing, 'sub', split_axis=0, concat_axis=0, tiled=True)  32.7 us
    another operation x4, other arithmetic, factor_and_inverse(): i22 = jax.scipy.linalg.solve_triangular(f22, identity, lower=True)  30.9 us
    another operation x6, other arithmetic, factor_and_inverse(): f22 = jnp.linalg.cholesky(schur[h:, h:] - _dot(f21, f21.T))  24.9 us
    another operation x6, other arithmetic, factor_and_inverse(): f11 = jnp.linalg.cholesky(schur[:h, :h])  24.8 us
    another operation x4, other arithmetic, factor_and_inverse(): i11 = jax.scipy.linalg.solve_triangular(f11, identity, lower=True)  20.9 us
    all_to_all x1, starting transfers between devices, body(): lax.all_to_all(outgoing, 'sub', split_axis=0, concat_axis=0, tiled=True)  7.4 us
  transfers between devices with their start and end apart: 1, of which 1 were waited for; matrix products, arithmetic and copies ran while one was open for 22% of the time, Pallas kernels for 0%

profile of v2, /device:TPU:64, one launch (start us, length us, event | category | flops | bytes accessed | tf_op | source)
XLA Modules:
  0.0 282.8 jit_solution(4747613662053852509)
XLA Ops:
  0.6 1.0 copy-done
  1.9 0.7 reshape.184.x_ref
  2.7 0.8 copy.32
  3.6 38.8 %shard_map.104 = f32[512,128]{1,0:T(8,128)} custom-call(f32[512,128]{1,0:T(8,128)} %reshape.184.x_ref), custom_call_target="tpu_custom_call" | custom-call | flops 262144 | bytes 786432 | tf_op jit(solution)/shard_map/pallas_call | solution.py:119
  42.4 1.0 reshape.185
  43.5 0.7 dynamic-slice_bitcast_fusion
  44.2 0.7 gather_fusion
  45.2 3.0 %broadcast_in_dim.97 = bf16[64,256,128]{2,1,0:T(8,128)(2,1)} broadcast(bf16[]{:T(256)} %constant.104.clone.1), dimensions={} | broadcast | bytes 4194306 | tf_op jit(solution)/shard_map/broadcast_in_dim | solution.py:303
  48.2 5.3 %scatter_fusion = bf16[64,256,128]{2,1,0:T(8,128)(2,1)} fusion(bf16[64,256,128]{2,1,0:T(8,128)(2,1)} %broadcast_in_dim.97, s32[24]{0:T(128)S(1)} %fusion.100, bf16[24,256,128]{2,1,0:T(8,128)(2,1)S(1)} %bitcast.129), kind=kCustom, calls=%fused_computation.4 | custom fusion | bytes 4718688 | tf_op jit(solution)/shard_map/scatter | solution.py:305
  53.5 7.4 %all-to-all-start = ((bf16[64,256,128]{2,1,0:T(8,128)(2,1)}), bf16[64,256,128]{2,1,0:T(8,128)(2,1)}, u32[]{:S(2)}, u32[]{:S(2)}) async-start(bf16[64,256,128]{2,1,0:T(8,128)(2,1)} %scatter_fusion), calls=%async_computation | async-start | bytes 8388608 | tf_op jit(solution)/shard_map/all_to_all | solution.py:307
  61.4 11.7 %cholesky.74 = f32[128,128]{1,0:T(8,128)S(1)} custom-call(f32[128,128]{1,0:T(8,128)S(1)} %fusion.85), custom_call_target="Cholesky" | custom-call | tf_op jit(solution)/shard_map/jit(cholesky)/cholesky | solution.py:247
  73.1 0.6 compare_reduce_fusion.3
  73.8 0.7 fusion.91
  74.4 9.8 %custom-call.12 = f32[1,128,128]{1,2,0:T(8,128)S(1)} custom-call(f32[1,128,128]{2,1,0:T(8,128)S(1)} %get-tuple-element.22), custom_call_target="InvertDiagBlocksLowerTriangular" | custom-call | tf_op jit(solution)/shard_map/jit(_solve_triangular)/triangular_solve | solution.py:248
  85.3 11.7 %cholesky.85 = f32[128,128]{1,0:T(8,128)S(1)} custom-call(f32[128,128]{1,0:T(8,128)S(1)} %fusion.83), custom_call_target="Cholesky" | custom-call | tf_op jit(solution)/shard_map/jit(cholesky)/cholesky | solution.py:250
  97.0 0.6 compare_reduce_fusion.2
  97.7 0.7 fusion.92
  98.3 19.8 %custom-call.13 = f32[1,128,128]{1,2,0:T(8,128)S(1)} custom-call(f32[1,128,128]{2,1,0:T(8,128)S(1)} %get-tuple-element.20), custom_call_target="InvertDiagBlocksLowerTriangular" | custom-call | tf_op jit(solution)/shard_map/jit(_solve_triangular)/triangular_solve | solution.py:251
  118.5 0.5 fusion.17
  119.0 2.3 gather_fusion.1
  121.9 0.6 fusion.36
  122.4 0.4 fusion.42
  123.2 0.7 fusion.30
  123.9 32.7 %all-to-all-done = bf16[64,256,128]{2,1,0:T(8,128)(2,1)} async-done(((bf16[64,256,128]{2,1,0:T(8,128)(2,1)}), bf16[64,256,128]{2,1,0:T(8,128)(2,1)}, u32[]{:S(2)}, u32[]{:S(2)}) %all-to-all-start) | async-done | bytes 4194336 | tf_op jit(solution)/shard_map/all_to_all | solution.py:307
  156.6 4.7 %fusion.8 = f32[256,256]{0,1:T(8,128)S(1)} fusion(bf16[64,256,128]{2,1,0:T(8,128)(2,1)} %all-to-all-done, f32[1,256,256]{1,2,0:T(8,128)S(1)} %copy.34), kind=kOutput, calls=%fused_computation.18 | convolution fusion | flops 1073807360 | bytes 4718592 | tf_op jit(solution)/shard_map/nbw,ncw->bc/dot_general | solution.py:309
  161.5 11.7 %cholesky.96 = f32[128,128]{1,0:T(8,128)S(1)} custom-call(f32[128,128]{1,0:T(8,128)S(1)} %fusion.81), custom_call_target="Cholesky" | custom-call | tf_op jit(solution)/shard_map/jit(cholesky)/cholesky | solution.py:247
  173.2 0.6 compare_reduce_fusion.1
  173.9 0.7 select_bitcast_fusion.1
  174.6 9.8 %custom-call.14 = f32[1,128,128]{1,2,0:T(8,128)S(1)} custom-call(f32[1,128,128]{2,1,0:T(8,128)S(1)} %get-tuple-element.18), custom_call_target="InvertDiagBlocksLowerTriangular" | custom-call | tf_op jit(solution)/shard_map/jit(_solve_triangular)/triangular_solve | solution.py:248
  185.4 11.9 %cholesky.107 = f32[128,128]{1,0:T(8,128)S(1)} custom-call(f32[128,128]{1,0:T(8,128)S(1)} %fusion.79), custom_call_target="Cholesky" | custom-call | tf_op jit(solution)/shard_map/jit(cholesky)/cholesky | solution.py:250
  197.3 0.6 compare_reduce_fusion
  197.9 0.7 select_bitcast_fusion
  198.6 9.8 %custom-call.15 = f32[1,128,128]{1,2,0:T(8,128)S(1)} custom-call(f32[1,128,128]{2,1,0:T(8,128)S(1)} %get-tuple-element.16), custom_call_target="InvertDiagBlocksLowerTriangular" | custom-call | tf_op jit(solution)/shard_map/jit(_solve_triangular)/triangular_solve | solution.py:251
  209.3 0.5 fusion.11
  209.8 2.3 gather_fusion.2
  212.2 0.6 fusion.31
  213.4 0.7 maximum_maximum_fusion.1.a_ref
  214.1 46.3 %shard_map.105 = bf16[32,272,128]{2,1,0:T(8,128)(2,1)} custom-call(bf16[272,128]{1,0:T(8,128)(2,1)} %maximum_maximum_fusion.1.a_ref), custom_call_target="tpu_custom_call" | custom-call | bytes 4456448 | tf_op jit(solution)/shard_map/pallas_call | solution.py:197
  260.4 2.5 slice.54
  262.8 0.8 slice.56
  263.7 2.3 copy.52
  266.0 3.0 %bitcast_select_fusion.1 = (bf16[32,128,128]{2,1,0:T(8,128)(2,1)}, bf16[32,128,128]{2,1,0:T(8,128)(2,1)}, bf16[32,128,128]{2,1,0:T(8,128)(2,1)}) fusion(bf16[32,128,128]{1,2,0:T(8,128)(2,1)} %copy.52, pred[128,128]{1,0:T(8,128)(4,1)S(1)} %iota_compare_fusion.16, bf16[32,272,128]{2,1,0:T(8,128)(2,1)S(1)} %copy-done.1, bf16[32,128]{1,0:T(8,128)(2,1)S(1)} %bitcast.131, ...), kind=kLoop, calls=%fused_computation.24 | loop fusion | flops 1572864 | bytes 6348800 | tf_op jit(solution)/shard_map/jit(_where)/select_n | solution.py:233
  269.0 1.6 copy.53
  270.6 3.6 %maximum_maximum_fusion = bf16[32,256,256]{2,1,0:T(8,128)(2,1)} fusion(bf16[32,128,128]{2,1,0:T(8,128)(2,1)} %get-tuple-element.25, bf16[32,128,128]{2,1,0:T(8,128)(2,1)} %get-tuple-element.26, bf16[32,128,128]{2,1,0:T(8,128)(2,1)S(1)} %bitcast.127, bf16[32,128,128]{2,1,0:T(8,128)(2,1)} %get-tuple-element.24), kind=kLoop, calls=%fused_computation.5 | loop fusion | flops 16777216 | bytes 8388608 | tf_op jit(solution)/shard_map/concatenate | solution.py:237
  274.2 2.9 %gather_fusion.3 = bf16[24,256,256]{2,1,0:T(8,128)(2,1)S(1)} fusion(bf16[32,256,256]{2,1,0:T(8,128)(2,1)} %maximum_maximum_fusion, s32[1024]{0:T(1024)S(1)} %pad_clamp_fusion), kind=kCustom, calls=%fused_computation.3 | custom fusion | bytes 6291552 | tf_op jit(solution)/shard_map/jit(_take)/gather | solution.py:312
  277.2 2.5 multiply_convert_fusion
  279.7 1.7 convolution_convert_fusion
  281.4 1.2 convolution_convert_fusion.1
  (76 shorter events, 6.1 us)
Async XLA Ops:
  0.6 1.0 copy-start
  1.9 46.3 %copy-start.2 = (bf16[6,4,256,128]{3,2,1,0:T(8,128)(2,1)S(1)}, bf16[6,4,256,128]{3,2,1,0:T(8,128)(2,1)}, u32[]{:S(2)}) copy-start(bf16[6,4,256,128]{3,2,1,0:T(8,128)(2,1)} %param.12) | copy-start | bytes 4718596
  53.5 7.6 %copy-start.6 = (f32[256,256]{1,0:T(8,128)S(1)}, f32[256,256]{1,0:T(8,128)}, u32[]{:S(2)}) copy-start(f32[256,256]{1,0:T(8,128)} %param.19) | copy-start | bytes 786436
  53.5 103.1 %all-to-all-start = ((bf16[64,256,128]{2,1,0:T(8,128)(2,1)}), bf16[64,256,128]{2,1,0:T(8,128)(2,1)}, u32[]{:S(2)}, u32[]{:S(2)}) async-start(bf16[64,256,128]{2,1,0:T(8,128)(2,1)} %scatter_fusion), calls=%async_computation | async-start | bytes 8388608 | tf_op jit(solution)/shard_map/all_to_all | solution.py:307
  60.9 57.6 %copy-start.8 = (f32[256,256]{1,0:T(8,128)S(1)}, f32[256,256]{1,0:T(8,128)}, u32[]{:S(2)}) copy-start(f32[256,256]{1,0:T(8,128)} %param.20) | copy-start | bytes 786436
  74.4 48.5 %copy-start.7 = (f32[1,256,256]{2,1,0:T(8,128)S(1)}, f32[1,256,256]{2,1,0:T(8,128)}, u32[]{:S(2)}) copy-start(f32[1,256,256]{2,1,0:T(8,128)} %param.17) | copy-start | bytes 786436
  123.9 85.4 %copy-start.9 = (f32[1,256,256]{2,1,0:T(8,128)S(1)}, f32[1,256,256]{2,1,0:T(8,128)}, u32[]{:S(2)}) copy-start(f32[1,256,256]{2,1,0:T(8,128)} %param.18) | copy-start | bytes 786436
  260.4 5.6 %copy-start.1 = (bf16[32,272,128]{2,1,0:T(8,128)(2,1)S(1)}, bf16[32,272,128]{2,1,0:T(8,128)(2,1)}, u32[]{:S(2)}) copy-start(bf16[32,272,128]{2,1,0:T(8,128)(2,1)} %shard_map.105) | copy-start | bytes 6684676
  277.2 2.5 copy-start.3
  279.6 1.7 copy-start.4
  279.7 1.7 copy-start.5

commit v3 on v2

--- a/solution.py
+++ b/solution.py
@@ -150,8 +150,10 @@
     sub = lax.axis_index("sub")
     x = sub // 8
     z = sub % 8
+    right = ((x + 1) % 4) * 8 + z
+    left = ((x + 3) % 4) * 8 + z
     peers = [(leaf, x * 8 + (z + d) % 8) for d in range(1, 8)]
-    peers += [(leaf, ((x + d) % 4) * 8 + z) for d in range(1, 4)]
+    peers += [(leaf, right), (leaf, left)]
     barrier = pltpu.get_barrier_semaphore()
     for p in peers:
         pl.semaphore_signal(barrier, inc=1, device_id=p, device_id_type=MESH)
@@ -180,13 +182,21 @@
         zz = (z + d) % 8
         recv_wait(gathered.at[x * 8 + zz], rsz.at[zz], (leaf, x * 8 + zz))
     own.wait()
-    column = gathered.at[pl.ds(pl.multiple_of(x * 8, 8), 8)]
-    for d in range(1, 4):
-        xx = (x + d) % 4
-        send(column, column, rsx.at[x], (leaf, xx * 8 + z))
-    for d in range(1, 4):
-        xx = (x + d) % 4
-        recv_wait(gathered.at[pl.ds(pl.multiple_of(xx * 8, 8), 8)], rsx.at[xx], (leaf, xx * 8 + z))
+
+    def column(xx, first, count):
+        return gathered.at[pl.ds(pl.multiple_of(xx * 8 + first, 4), count)]
+
+    x_left = (x + 3) % 4
+    x_right = (x + 1) % 4
+    x_far = (x + 2) % 4
+    send(column(x, 0, 8), column(x, 0, 8), rsx.at[0], (leaf, right))
+    send(column(x, 0, 8), column(x, 0, 8), rsx.at[1], (leaf, left))
+    recv_wait(column(x_left, 0, 8), rsx.at[0], (leaf, left))
+    send(column(x_left, 0, 4), column(x_left, 0, 4), rsx.at[2], (leaf, right))
+    recv_wait(column(x_right, 0, 8), rsx.at[1], (leaf, right))
+    send(column(x_right, 4, 4), column(x_right, 4, 4), rsx.at[3], (leaf, left))
+    recv_wait(column(x_far, 0, 4), rsx.at[2], (leaf, left))
+    recv_wait(column(x_far, 4, 4), rsx.at[3], (leaf, right))
     for cp in sends:
         cp.wait_send()
     o_ref[...] = gathered[...]
@@ -201,7 +211,7 @@
         out_specs=pl.BlockSpec(memory_space=pltpu.VMEM),
         scratch_shapes=[
             pltpu.VMEM((32, rows, 128), block.dtype),
-            pltpu.SemaphoreType.DMA((10,)),
+            pltpu.SemaphoreType.DMA((11,)),
             pltpu.SemaphoreType.DMA((8,)),
             pltpu.SemaphoreType.DMA((4,)),
             pltpu.SemaphoreType.DMA((1,)),

time: 286 us -> 281 us (0.983)
  the two profiles are of different devices: /device:TPU:64 before, /device:TPU:128 now
where the time goes in v3:
time: 281 us; the launch traced here: 278 us
  other arithmetic  110 us (39%)
  Pallas kernels  80.9 us (29%)
  waiting for transfers between devices  31.9 us (11%)
  local copies, waits for them, and re-layouts  29.8 us (11%)
  matrix products  16.4 us (6%)
  starting transfers between devices  7.23 us (3%)
    pallas_call x1, Pallas kernels, gather_sub(): pl.pallas_call(_gather_kernel, out_shape=jax.ShapeDtypeStruct((32, rows,...  42.9 us
    pallas_call x1, Pallas kernels, allreduce_root(): pl.pallas_call(_allreduce_kernel, out_shape=jax.ShapeDtypeStruct((512, 12...  38 us
    all_to_all x1, waiting for transfers between devices, body(): lax.all_to_all(outgoing, 'sub', split_axis=0, concat_axis=0, tiled=True)  31.9 us
    another operation x4, other arithmetic, factor_and_inverse(): i22 = jax.scipy.linalg.solve_triangular(f22, identity, lower=True)  30.9 us
    another operation x6, other arithmetic, factor_and_inverse(): f22 = jnp.linalg.cholesky(schur[h:, h:] - _dot(f21, f21.T))  24.9 us
    another operation x6, other arithmetic, factor_and_inverse(): f11 = jnp.linalg.cholesky(schur[:h, :h])  24.8 us
    another operation x4, other arithmetic, factor_and_inverse(): i11 = jax.scipy.linalg.solve_triangular(f11, identity, lower=True)  20.9 us
    all_to_all x1, starting transfers between devices, body(): lax.all_to_all(outgoing, 'sub', split_axis=0, concat_axis=0, tiled=True)  7.23 us
  transfers between devices with their start and end apart: 1, of which 1 were waited for; matrix products, arithmetic and copies ran while one was open for 23% of the time, Pallas kernels for 0%

profile of v3, /device:TPU:128, one launch (start us, length us, event | category | flops | bytes accessed | tf_op | source)
XLA Modules:
  0.0 277.8 jit_solution(11056567113499954471)
XLA Ops:
  0.6 1.0 copy-done
  1.9 0.7 reshape.184.x_ref
  2.7 0.8 copy.32
  3.6 38.0 %shard_map.104 = f32[512,128]{1,0:T(8,128)} custom-call(f32[512,128]{1,0:T(8,128)} %reshape.184.x_ref), custom_call_target="tpu_custom_call" | custom-call | flops 262144 | bytes 786432 | tf_op jit(solution)/shard_map/pallas_call | solution.py:119
  41.6 1.0 reshape.185
  42.7 0.7 dynamic-slice_bitcast_fusion
  43.4 0.7 gather_fusion
  44.4 3.0 %broadcast_in_dim.97 = bf16[64,256,128]{2,1,0:T(8,128)(2,1)} broadcast(bf16[]{:T(256)} %constant.104.clone.1), dimensions={} | broadcast | bytes 4194306 | tf_op jit(solution)/shard_map/broadcast_in_dim | solution.py:313
  47.4 5.4 %scatter_fusion = bf16[64,256,128]{2,1,0:T(8,128)(2,1)} fusion(bf16[64,256,128]{2,1,0:T(8,128)(2,1)} %broadcast_in_dim.97, s32[24]{0:T(128)S(1)} %fusion.100, bf16[24,256,128]{2,1,0:T(8,128)(2,1)S(1)} %bitcast.129), kind=kCustom, calls=%fused_computation.4 | custom fusion | bytes 4718688 | tf_op jit(solution)/shard_map/scatter | solution.py:315
  52.8 7.2 %all-to-all-start = ((bf16[64,256,128]{2,1,0:T(8,128)(2,1)}), bf16[64,256,128]{2,1,0:T(8,128)(2,1)}, u32[]{:S(2)}, u32[]{:S(2)}) async-start(bf16[64,256,128]{2,1,0:T(8,128)(2,1)} %scatter_fusion), calls=%async_computation | async-start | bytes 8388608 | tf_op jit(solution)/shard_map/all_to_all | solution.py:317
  60.5 11.7 %cholesky.74 = f32[128,128]{1,0:T(8,128)S(1)} custom-call(f32[128,128]{1,0:T(8,128)S(1)} %fusion.85), custom_call_target="Cholesky" | custom-call | tf_op jit(solution)/shard_map/jit(cholesky)/cholesky | solution.py:257
  72.3 0.6 compare_reduce_fusion.3
  72.9 0.7 fusion.91
  73.6 9.8 %custom-call.12 = f32[1,128,128]{1,2,0:T(8,128)S(1)} custom-call(f32[1,128,128]{2,1,0:T(8,128)S(1)} %get-tuple-element.22), custom_call_target="InvertDiagBlocksLowerTriangular" | custom-call | tf_op jit(solution)/shard_map/jit(_solve_triangular)/triangular_solve | solution.py:258
  84.4 11.7 %cholesky.85 = f32[128,128]{1,0:T(8,128)S(1)} custom-call(f32[128,128]{1,0:T(8,128)S(1)} %fusion.83), custom_call_target="Cholesky" | custom-call | tf_op jit(solution)/shard_map/jit(cholesky)/cholesky | solution.py:260
  96.2 0.6 compare_reduce_fusion.2
  96.8 0.7 fusion.92
  97.5 19.8 %custom-call.13 = f32[1,128,128]{1,2,0:T(8,128)S(1)} custom-call(f32[1,128,128]{2,1,0:T(8,128)S(1)} %get-tuple-element.20), custom_call_target="InvertDiagBlocksLowerTriangular" | custom-call | tf_op jit(solution)/shard_map/jit(_solve_triangular)/triangular_solve | solution.py:261
  117.6 0.5 fusion.17
  118.1 2.3 gather_fusion.1
  121.0 0.6 fusion.36
  122.4 0.7 fusion.30
  123.1 31.9 %all-to-all-done = bf16[64,256,128]{2,1,0:T(8,128)(2,1)} async-done(((bf16[64,256,128]{2,1,0:T(8,128)(2,1)}), bf16[64,256,128]{2,1,0:T(8,128)(2,1)}, u32[]{:S(2)}, u32[]{:S(2)}) %all-to-all-start) | async-done | bytes 4194336 | tf_op jit(solution)/shard_map/all_to_all | solution.py:317
  155.0 4.7 %fusion.8 = f32[256,256]{0,1:T(8,128)S(1)} fusion(bf16[64,256,128]{2,1,0:T(8,128)(2,1)} %all-to-all-done, f32[1,256,256]{1,2,0:T(8,128)S(1)} %copy.34), kind=kOutput, calls=%fused_computation.18 | convolution fusion | flops 1073807360 | bytes 4718592 | tf_op jit(solution)/shard_map/nbw,ncw->bc/dot_general | solution.py:319
  159.9 11.7 %cholesky.96 = f32[128,128]{1,0:T(8,128)S(1)} custom-call(f32[128,128]{1,0:T(8,128)S(1)} %fusion.81), custom_call_target="Cholesky" | custom-call | tf_op jit(solution)/shard_map/jit(cholesky)/cholesky | solution.py:257
  171.6 0.6 compare_reduce_fusion.1
  172.2 0.7 select_bitcast_fusion.1
  172.9 9.8 %custom-call.14 = f32[1,128,128]{1,2,0:T(8,128)S(1)} custom-call(f32[1,128,128]{2,1,0:T(8,128)S(1)} %get-tuple-element.18), custom_call_target="InvertDiagBlocksLowerTriangular" | custom-call | tf_op jit(solution)/shard_map/jit(_solve_triangular)/triangular_solve | solution.py:258
  183.7 11.9 %cholesky.107 = f32[128,128]{1,0:T(8,128)S(1)} custom-call(f32[128,128]{1,0:T(8,128)S(1)} %fusion.79), custom_call_target="Cholesky" | custom-call | tf_op jit(solution)/shard_map/jit(cholesky)/cholesky | solution.py:260
  195.7 0.6 compare_reduce_fusion
  196.3 0.7 select_bitcast_fusion
  197.0 9.8 %custom-call.15 = f32[1,128,128]{1,2,0:T(8,128)S(1)} custom-call(f32[1,128,128]{2,1,0:T(8,128)S(1)} %get-tuple-element.16), custom_call_target="InvertDiagBlocksLowerTriangular" | custom-call | tf_op jit(solution)/shard_map/jit(_solve_triangular)/triangular_solve | solution.py:261
  207.7 0.5 fusion.11
  208.2 2.3 gather_fusion.2
  210.5 0.6 fusion.31
  211.1 0.4 fusion.45
  211.7 0.7 maximum_maximum_fusion.1.a_ref
  212.4 42.9 %shard_map.105 = bf16[32,272,128]{2,1,0:T(8,128)(2,1)} custom-call(bf16[272,128]{1,0:T(8,128)(2,1)} %maximum_maximum_fusion.1.a_ref), custom_call_target="tpu_custom_call" | custom-call | bytes 4456448 | tf_op jit(solution)/shard_map/pallas_call | solution.py:207
  255.4 2.5 slice.54
  257.8 0.8 slice.56
  258.7 2.3 copy.52
  261.0 3.0 %bitcast_select_fusion.1 = (bf16[32,128,128]{2,1,0:T(8,128)(2,1)}, bf16[32,128,128]{2,1,0:T(8,128)(2,1)}, bf16[32,128,128]{2,1,0:T(8,128)(2,1)}) fusion(bf16[32,128,128]{1,2,0:T(8,128)(2,1)} %copy.52, pred[128,128]{1,0:T(8,128)(4,1)S(1)} %iota_compare_fusion.16, bf16[32,272,128]{2,1,0:T(8,128)(2,1)S(1)} %copy-done.1, bf16[32,128]{1,0:T(8,128)(2,1)S(1)} %bitcast.131, ...), kind=kLoop, calls=%fused_computation.24 | loop fusion | flops 1572864 | bytes 6348800 | tf_op jit(solution)/shard_map/jit(_where)/select_n | solution.py:243
  264.0 1.6 copy.53
  265.6 3.6 %maximum_maximum_fusion = bf16[32,256,256]{2,1,0:T(8,128)(2,1)} fusion(bf16[32,128,128]{2,1,0:T(8,128)(2,1)} %get-tuple-element.25, bf16[32,128,128]{2,1,0:T(8,128)(2,1)} %get-tuple-element.26, bf16[32,128,128]{2,1,0:T(8,128)(2,1)S(1)} %bitcast.127, bf16[32,128,128]{2,1,0:T(8,128)(2,1)} %get-tuple-element.24), kind=kLoop, calls=%fused_computation.5 | loop fusion | flops 16777216 | bytes 8388608 | tf_op jit(solution)/shard_map/concatenate | solution.py:247
  269.2 2.9 %gather_fusion.3 = bf16[24,256,256]{2,1,0:T(8,128)(2,1)S(1)} fusion(bf16[32,256,256]{2,1,0:T(8,128)(2,1)} %maximum_maximum_fusion, s32[1024]{0:T(1024)S(1)} %pad_clamp_fusion), kind=kCustom, calls=%fused_computation.3 | custom fusion | bytes 6291552 | tf_op jit(solution)/shard_map/jit(_take)/gather | solution.py:322
  272.1 2.5 multiply_convert_fusion
  274.7 1.7 convolution_convert_fusion
  276.4 1.2 convolution_convert_fusion.1
  (76 shorter events, 6.1 us)
Async XLA Ops:
  0.6 1.0 copy-start
  1.9 45.5 %copy-start.2 = (bf16[6,4,256,128]{3,2,1,0:T(8,128)(2,1)S(1)}, bf16[6,4,256,128]{3,2,1,0:T(8,128)(2,1)}, u32[]{:S(2)}) copy-start(bf16[6,4,256,128]{3,2,1,0:T(8,128)(2,1)} %param.12) | copy-start | bytes 4718596
  52.8 7.4 %copy-start.6 = (f32[256,256]{1,0:T(8,128)S(1)}, f32[256,256]{1,0:T(8,128)}, u32[]{:S(2)}) copy-start(f32[256,256]{1,0:T(8,128)} %param.19) | copy-start | bytes 786436
  52.8 102.2 %all-to-all-start = ((bf16[64,256,128]{2,1,0:T(8,128)(2,1)}), bf16[64,256,128]{2,1,0:T(8,128)(2,1)}, u32[]{:S(2)}, u32[]{:S(2)}) async-start(bf16[64,256,128]{2,1,0:T(8,128)(2,1)} %scatter_fusion), calls=%async_computation | async-start | bytes 8388608 | tf_op jit(solution)/shard_map/all_to_all | solution.py:317
  60.1 57.6 %copy-start.8 = (f32[256,256]{1,0:T(8,128)S(1)}, f32[256,256]{1,0:T(8,128)}, u32[]{:S(2)}) copy-start(f32[256,256]{1,0:T(8,128)} %param.20) | copy-start | bytes 786436
  73.6 48.5 %copy-start.7 = (f32[1,256,256]{2,1,0:T(8,128)S(1)}, f32[1,256,256]{2,1,0:T(8,128)}, u32[]{:S(2)}) copy-start(f32[1,256,256]{2,1,0:T(8,128)} %param.17) | copy-start | bytes 786436
  123.1 84.6 %copy-start.9 = (f32[1,256,256]{2,1,0:T(8,128)S(1)}, f32[1,256,256]{2,1,0:T(8,128)}, u32[]{:S(2)}) copy-start(f32[1,256,256]{2,1,0:T(8,128)} %param.18) | copy-start | bytes 786436
  255.3 5.6 %copy-start.1 = (bf16[32,272,128]{2,1,0:T(8,128)(2,1)S(1)}, bf16[32,272,128]{2,1,0:T(8,128)(2,1)}, u32[]{:S(2)}) copy-start(bf16[32,272,128]{2,1,0:T(8,128)(2,1)} %shard_map.105) | copy-start | bytes 6684676
  272.1 2.5 copy-start.3
  274.6 1.7 copy-start.4
  274.6 1.7 copy-start.5

commit v4 on v3

--- a/solution.py
+++ b/solution.py
@@ -266,6 +266,35 @@
     return factor, inverse
 
 
+def packed_times(packed, panels):
+    h = 128
+    folded = packed[:, :h, :]
+    lower = packed[:, h:2 * h, :]
+    diag_col = jnp.swapaxes(packed[:, 2 * h:2 * h + 1, :], 1, 2).astype(jnp.float32)
+    row = lax.broadcasted_iota(jnp.int32, (1, h, h), 1)
+    col = lax.broadcasted_iota(jnp.int32, (1, h, h), 2)
+    zero = jnp.zeros_like(folded)
+    low_incl = jnp.where(col <= row, folded, zero)
+    low_strict = jnp.where(col < row, folded, zero)
+    up_strict = jnp.where(col > row, folded, zero)
+    top_in, bottom_in = panels[:, :h, :], panels[:, h:, :]
+
+    def mul(a, b):
+        return jnp.einsum("nbk,nkw->nbw", a, b, preferred_element_type=jnp.float32)
+
+    def mul_t(a, b):
+        return jnp.einsum("nkb,nkw->nbw", a, b, preferred_element_type=jnp.float32)
+
+    top = mul(low_incl, top_in) + mul_t(low_strict, top_in) + mul_t(lower, bottom_in)
+    bottom = (
+        mul(lower, top_in)
+        + mul(up_strict, bottom_in)
+        + mul_t(up_strict, bottom_in)
+        + diag_col * bottom_in.astype(jnp.float32)
+    )
+    return jnp.concatenate([top, bottom], axis=1)
+
+
 def adjoint_block(schur, cotangent):
     factor, inverse = factor_and_inverse(schur)
     product = jnp.dot(factor.T, cotangent, precision=lax.Precision.HIGHEST)
@@ -318,12 +347,8 @@
     root_adjoint, incoming = lax.optimization_barrier((root_adjoint, incoming))
     gram_sum = jnp.einsum("nbw,ncw->bc", incoming, incoming, preferred_element_type=jnp.float32)
     upper_adjoint = adjoint_block(upper_block[0] - gram_sum, upper_cot[0])
-    every_adjoint = unpack_symmetric(gather_sub(pack_symmetric(upper_adjoint)))
-    chosen = jnp.take(every_adjoint, target, axis=0)
-    panel_adjoint = (
-        -2.0
-        * jnp.einsum("nbc,ncw->nbw", chosen, flat_panels, preferred_element_type=jnp.float32)
-    ).astype(jnp.bfloat16)
+    chosen = jnp.take(gather_sub(pack_symmetric(upper_adjoint)), target, axis=0)
+    panel_adjoint = (-2.0 * packed_times(chosen, flat_panels)).astype(jnp.bfloat16)
     panel_adjoint = panel_adjoint.reshape(rows_dev, blocks_row, height, breadth)
     panel_grad = jnp.einsum(
         "srbw,swv->srbv", panel_adjoint, low_inverse, preferred_element_type=jnp.float32

time: 281 us -> 275 us (0.979)
  the two profiles are of different devices: /device:TPU:128 before, /device:TPU:64 now
where the time goes in v4:
time: 275 us; the launch traced here: 272 us
  other arithmetic  107 us (39%)
  Pallas kernels  79.9 us (29%)
  waiting for transfers between devices  31.6 us (11%)
  local copies, waits for them, and re-layouts  22.9 us (8%)
  matrix products  21.8 us (8%)
  starting transfers between devices  7.32 us (3%)
    pallas_call x1, Pallas kernels, gather_sub(): pl.pallas_call(_gather_kernel, out_shape=jax.ShapeDtypeStruct((32, rows,...  41.1 us
    pallas_call x1, Pallas kernels, allreduce_root(): pl.pallas_call(_allreduce_kernel, out_shape=jax.ShapeDtypeStruct((512, 12...  38.8 us
    all_to_all x1, waiting for transfers between devices, body(): lax.all_to_all(outgoing, 'sub', split_axis=0, concat_axis=0, tiled=True)  31.6 us
    another operation x4, other arithmetic, factor_and_inverse(): i22 = jax.scipy.linalg.solve_triangular(f22, identity, lower=True)  30.9 us
    another operation x6, other arithmetic, factor_and_inverse(): f22 = jnp.linalg.cholesky(schur[h:, h:] - _dot(f21, f21.T))  24.9 us
    another operation x6, other arithmetic, factor_and_inverse(): f11 = jnp.linalg.cholesky(schur[:h, :h])  24.8 us
    another operation x4, other arithmetic, factor_and_inverse(): i11 = jax.scipy.linalg.solve_triangular(f11, identity, lower=True)  20.9 us
    all_to_all x1, starting transfers between devices, body(): lax.all_to_all(outgoing, 'sub', split_axis=0, concat_axis=0, tiled=True)  7.32 us
  transfers between devices with their start and end apart: 1, of which 1 were waited for; matrix products, arithmetic and copies ran while one was open for 23% of the time, Pallas kernels for 0%

profile of v4, /device:TPU:64, one launch (start us, length us, event | category | flops | bytes accessed | tf_op | source)
XLA Modules:
  0.0 272.1 jit_solution(13059535572250393674)
XLA Ops:
  0.7 1.0 copy-done
  1.9 0.7 reshape.193.x_ref
  2.9 38.8 %shard_map.104 = f32[512,128]{1,0:T(8,128)} custom-call(f32[512,128]{1,0:T(8,128)} %reshape.193.x_ref), custom_call_target="tpu_custom_call" | custom-call | flops 262144 | bytes 786432 | tf_op jit(solution)/shard_map/pallas_call | solution.py:119
  41.7 1.0 reshape.194
  42.8 0.7 dynamic-slice_bitcast_fusion
  43.5 0.7 gather_fusion
  44.5 3.0 %broadcast_in_dim.87 = bf16[64,256,128]{2,1,0:T(8,128)(2,1)} broadcast(bf16[]{:T(256)} %constant.105.clone.1), dimensions={} | broadcast | bytes 4194306 | tf_op jit(solution)/shard_map/broadcast_in_dim | solution.py:342
  47.5 5.4 %scatter_fusion = bf16[64,256,128]{2,1,0:T(8,128)(2,1)} fusion(bf16[64,256,128]{2,1,0:T(8,128)(2,1)} %broadcast_in_dim.87, s32[24]{0:T(128)S(1)} %fusion.120, bf16[24,256,128]{2,1,0:T(8,128)(2,1)S(1)} %bitcast.118), kind=kCustom, calls=%fused_computation.4 | custom fusion | bytes 4718688 | tf_op jit(solution)/shard_map/scatter | solution.py:344
  52.9 7.3 %all-to-all-start = ((bf16[64,256,128]{2,1,0:T(8,128)(2,1)}), bf16[64,256,128]{2,1,0:T(8,128)(2,1)}, u32[]{:S(2)}, u32[]{:S(2)}) async-start(bf16[64,256,128]{2,1,0:T(8,128)(2,1)} %scatter_fusion), calls=%async_computation | async-start | bytes 8388608 | tf_op jit(solution)/shard_map/all_to_all | solution.py:346
  60.7 11.7 %cholesky.74 = f32[128,128]{1,0:T(8,128)S(1)} custom-call(f32[128,128]{1,0:T(8,128)S(1)} %fusion.105), custom_call_target="Cholesky" | custom-call | tf_op jit(solution)/shard_map/jit(cholesky)/cholesky | solution.py:257
  72.5 0.6 compare_reduce_fusion.3
  73.1 0.7 fusion.111
  73.8 9.8 %custom-call.12 = f32[1,128,128]{1,2,0:T(8,128)S(1)} custom-call(f32[1,128,128]{2,1,0:T(8,128)S(1)} %get-tuple-element.22), custom_call_target="InvertDiagBlocksLowerTriangular" | custom-call | tf_op jit(solution)/shard_map/jit(_solve_triangular)/triangular_solve | solution.py:258
  84.6 11.7 %cholesky.85 = f32[128,128]{1,0:T(8,128)S(1)} custom-call(f32[128,128]{1,0:T(8,128)S(1)} %fusion.103), custom_call_target="Cholesky" | custom-call | tf_op jit(solution)/shard_map/jit(cholesky)/cholesky | solution.py:260
  96.4 0.6 compare_reduce_fusion.2
  97.0 0.7 fusion.112
  97.7 19.7 %custom-call.13 = f32[1,128,128]{1,2,0:T(8,128)S(1)} custom-call(f32[1,128,128]{2,1,0:T(8,128)S(1)} %get-tuple-element.20), custom_call_target="InvertDiagBlocksLowerTriangular" | custom-call | tf_op jit(solution)/shard_map/jit(_solve_triangular)/triangular_solve | solution.py:261
  117.8 0.5 fusion.37
  118.3 2.3 gather_fusion.1
  121.2 0.6 fusion.56
  121.8 0.4 fusion.62
  122.5 0.6 iota_compare_fusion.15
  123.1 0.6 iota_compare_fusion.16
  123.8 0.7 fusion.50
  124.5 31.6 %all-to-all-done = bf16[64,256,128]{2,1,0:T(8,128)(2,1)} async-done(((bf16[64,256,128]{2,1,0:T(8,128)(2,1)}), bf16[64,256,128]{2,1,0:T(8,128)(2,1)}, u32[]{:S(2)}, u32[]{:S(2)}) %all-to-all-start) | async-done | bytes 4194336 | tf_op jit(solution)/shard_map/all_to_all | solution.py:346
  156.1 4.7 %fusion.5 = f32[256,256]{0,1:T(8,128)S(1)} fusion(bf16[64,256,128]{2,1,0:T(8,128)(2,1)} %all-to-all-done, f32[1,256,256]{1,2,0:T(8,128)S(1)} %copy.35), kind=kOutput, calls=%fused_computation.18 | convolution fusion | flops 1073807360 | bytes 4718592 | tf_op jit(solution)/shard_map/nbw,ncw->bc/dot_general | solution.py:348
  161.0 11.7 %cholesky.96 = f32[128,128]{1,0:T(8,128)S(1)} custom-call(f32[128,128]{1,0:T(8,128)S(1)} %fusion.101), custom_call_target="Cholesky" | custom-call | tf_op jit(solution)/shard_map/jit(cholesky)/cholesky | solution.py:257
  172.7 0.6 compare_reduce_fusion.1
  173.3 0.7 select_bitcast_fusion.1
  174.0 9.8 %custom-call.14 = f32[1,128,128]{1,2,0:T(8,128)S(1)} custom-call(f32[1,128,128]{2,1,0:T(8,128)S(1)} %get-tuple-element.18), custom_call_target="InvertDiagBlocksLowerTriangular" | custom-call | tf_op jit(solution)/shard_map/jit(_solve_triangular)/triangular_solve | solution.py:258
  184.8 11.8 %cholesky.107 = f32[128,128]{1,0:T(8,128)S(1)} custom-call(f32[128,128]{1,0:T(8,128)S(1)} %fusion.99), custom_call_target="Cholesky" | custom-call | tf_op jit(solution)/shard_map/jit(cholesky)/cholesky | solution.py:260
  196.7 0.6 compare_reduce_fusion
  197.4 0.7 select_bitcast_fusion
  198.0 9.8 %custom-call.15 = f32[1,128,128]{1,2,0:T(8,128)S(1)} custom-call(f32[1,128,128]{2,1,0:T(8,128)S(1)} %get-tuple-element.16), custom_call_target="InvertDiagBlocksLowerTriangular" | custom-call | tf_op jit(solution)/shard_map/jit(_solve_triangular)/triangular_solve | solution.py:261
  208.7 0.5 fusion.31
  209.2 2.3 gather_fusion.2
  211.6 0.6 fusion.51
  212.8 0.7 maximum_maximum_fusion.a_ref
  213.5 41.1 %shard_map.105 = bf16[32,272,128]{2,1,0:T(8,128)(2,1)} custom-call(bf16[272,128]{1,0:T(8,128)(2,1)} %maximum_maximum_fusion.a_ref), custom_call_target="tpu_custom_call" | custom-call | bytes 4456448 | tf_op jit(solution)/shard_map/pallas_call | solution.py:207
  254.6 3.6 %gather_fusion.3 = bf16[24,272,128]{2,1,0:T(8,128)(2,1)} fusion(bf16[32,272,128]{2,1,0:T(8,128)(2,1)} %shard_map.105, s32[1024]{0:T(1024)S(1)} %pad_clamp_fusion), kind=kCustom, calls=%fused_computation.3 | custom fusion | bytes 3342432 | tf_op jit(solution)/shard_map/jit(_take)/gather | solution.py:350
  258.2 1.7 broadcast_select_fusion
  260.3 0.8 slice_convert_fusion
  261.1 0.4 fusion.6
  262.2 1.5 fusion.15
  263.7 1.7 add_add_fusion
  265.4 2.2 convolution_convert_fusion.1
  267.6 2.5 multiply_add_fusion
  270.1 1.7 convolution_convert_fusion
  (81 shorter events, 7.2 us)
Async XLA Ops:
  0.6 1.0 copy-start
  0.6 2.0 copy-start.11
  44.5 3.0 %copy-start.1 = (bf16[6,4,256,128]{3,2,1,0:T(8,128)(2,1)S(1)}, bf16[6,4,256,128]{3,2,1,0:T(8,128)(2,1)}, u32[]{:S(2)}) copy-start(bf16[6,4,256,128]{3,2,1,0:T(8,128)(2,1)} %param.12) | copy-start | bytes 4718596
  52.9 7.5 %copy-start.5 = (f32[256,256]{1,0:T(8,128)S(1)}, f32[256,256]{1,0:T(8,128)}, u32[]{:S(2)}) copy-start(f32[256,256]{1,0:T(8,128)} %param.19) | copy-start | bytes 786436
  52.9 103.1 %all-to-all-start = ((bf16[64,256,128]{2,1,0:T(8,128)(2,1)}), bf16[64,256,128]{2,1,0:T(8,128)(2,1)}, u32[]{:S(2)}, u32[]{:S(2)}) async-start(bf16[64,256,128]{2,1,0:T(8,128)(2,1)} %scatter_fusion), calls=%async_computation | async-start | bytes 8388608 | tf_op jit(solution)/shard_map/all_to_all | solution.py:346
  60.5 57.3 %copy-start.7 = (f32[256,256]{1,0:T(8,128)S(1)}, f32[256,256]{1,0:T(8,128)}, u32[]{:S(2)}) copy-start(f32[256,256]{1,0:T(8,128)} %param.20) | copy-start | bytes 786436
  120.7 1.6 copy-start.6
  160.8 47.9 %copy-start.8 = (f32[1,256,256]{2,1,0:T(8,128)S(1)}, f32[1,256,256]{2,1,0:T(8,128)}, u32[]{:S(2)}) copy-start(f32[1,256,256]{2,1,0:T(8,128)} %param.18) | copy-start | bytes 786436
  259.9 3.8 %copy-start.2 = (bf16[24,272,128]{2,1,0:T(8,128)(2,1)}, bf16[24,272,128]{2,1,0:T(8,128)(2,1)S(1)}, u32[]{:S(2)}) copy-start(bf16[24,272,128]{2,1,0:T(8,128)(2,1)S(1)} %broadcast_select_fusion) | copy-start | bytes 5013508
  259.9 1.2 copy-start.10
  261.1 0.7 copy-start.9
  267.6 2.5 copy-start.3
  267.6 2.5 copy-start.4

commit v5 on v4

--- a/solution.py
+++ b/solution.py
@@ -338,13 +338,19 @@
     slot_id = jnp.sum(earlier * onehot, axis=1)
     position = target * capacity + slot_id
     flat_panels = panels.reshape(item_count, height, breadth)
-    outgoing = (
-        jnp.zeros((devices_sub * capacity, height, breadth), jnp.bfloat16)
-        .at[position]
-        .set(flat_panels)
-    )
+    slots = jnp.arange(devices_sub * capacity, dtype=jnp.int32)
+    match = position[None, :] == slots[:, None]
+    source = jnp.where(jnp.any(match, axis=1), jnp.argmax(match, axis=1), item_count)
+    outgoing = jnp.take(flat_panels, source, axis=0, mode="fill", fill_value=0)
     incoming = lax.all_to_all(outgoing, "sub", split_axis=0, concat_axis=0, tiled=True)
-    root_adjoint, incoming = lax.optimization_barrier((root_adjoint, incoming))
+    root_panel_adjoint = (
+        -2.0
+        * jnp.einsum("bc,scw->sbw", root_adjoint, root_panels, preferred_element_type=jnp.float32)
+    ).astype(jnp.bfloat16)
+    root_grad = jnp.einsum(
+        "sbw,swv->sbv", root_panel_adjoint, low_inverse, preferred_element_type=jnp.float32
+    ).astype(jnp.bfloat16)
+    root_grad, incoming = lax.optimization_barrier((root_grad, incoming))
     gram_sum = jnp.einsum("nbw,ncw->bc", incoming, incoming, preferred_element_type=jnp.float32)
     upper_adjoint = adjoint_block(upper_block[0] - gram_sum, upper_cot[0])
     chosen = jnp.take(gather_sub(pack_symmetric(upper_adjoint)), target, axis=0)
@@ -352,13 +358,6 @@
     panel_adjoint = panel_adjoint.reshape(rows_dev, blocks_row, height, breadth)
     panel_grad = jnp.einsum(
         "srbw,swv->srbv", panel_adjoint, low_inverse, preferred_element_type=jnp.float32
-    ).astype(jnp.bfloat16)
-    root_panel_adjoint = (
-        -2.0
-        * jnp.einsum("bc,scw->sbw", root_adjoint, root_panels, preferred_element_type=jnp.float32)
-    ).astype(jnp.bfloat16)
-    root_grad = jnp.einsum(
-        "sbw,swv->sbv", root_panel_adjoint, low_inverse, preferred_element_type=jnp.float32
     ).astype(jnp.bfloat16)
     return (panel_grad, root_grad)
 

time: 275 us -> 268 us (0.975)
  the two profiles are of different devices: /device:TPU:64 before, /device:TPU:128 now
where the time goes in v5:
time: 268 us; the launch traced here: 265 us
  other arithmetic  110 us (41%)
  Pallas kernels  81.4 us (30%)
  waiting for transfers between devices  31 us (12%)
  local copies, waits for them, and re-layouts  17 us (6%)
  matrix products  16.8 us (6%)
  starting transfers between devices  7.24 us (3%)
    pallas_call x1, Pallas kernels, gather_sub(): pl.pallas_call(_gather_kernel, out_shape=jax.ShapeDtypeStruct((32, rows,...  43.4 us
    pallas_call x1, Pallas kernels, allreduce_root(): pl.pallas_call(_allreduce_kernel, out_shape=jax.ShapeDtypeStruct((512, 12...  38 us
    all_to_all x1, waiting for transfers between devices, body(): lax.all_to_all(outgoing, 'sub', split_axis=0, concat_axis=0, tiled=True)  31 us
    another operation x4, other arithmetic, factor_and_inverse(): i22 = jax.scipy.linalg.solve_triangular(f22, identity, lower=True)  30.9 us
    another operation x6, other arithmetic, factor_and_inverse(): f22 = jnp.linalg.cholesky(schur[h:, h:] - _dot(f21, f21.T))  24.9 us
    another operation x6, other arithmetic, factor_and_inverse(): f11 = jnp.linalg.cholesky(schur[:h, :h])  24.8 us
    another operation x4, other arithmetic, factor_and_inverse(): i11 = jax.scipy.linalg.solve_triangular(f11, identity, lower=True)  20.9 us
    all_to_all x1, starting transfers between devices, body(): lax.all_to_all(outgoing, 'sub', split_axis=0, concat_axis=0, tiled=True)  7.24 us
  transfers between devices with their start and end apart: 1, of which 1 were waited for; matrix products, arithmetic and copies ran while one was open for 24% of the time, Pallas kernels for 0%

profile of v5, /device:TPU:128, one launch (start us, length us, event | category | flops | bytes accessed | tf_op | source)
XLA Modules:
  0.0 264.6 jit_solution(17741129803669549694)
XLA Ops:
  0.6 0.8 copy.56
  1.6 0.7 dynamic-slice_bitcast_fusion
  2.3 0.7 gather_fusion
  3.4 0.6 iota_reduce_fusion
  4.4 0.7 reshape.188.x_ref
  5.1 38.0 %shard_map.104 = f32[512,128]{1,0:T(8,128)} custom-call(f32[512,128]{1,0:T(8,128)} %reshape.188.x_ref), custom_call_target="tpu_custom_call" | custom-call | flops 262144 | bytes 786432 | tf_op jit(solution)/shard_map/pallas_call | solution.py:119
  43.1 1.0 reshape.189
  44.2 3.1 %gather_fusion.2 = bf16[64,256,128]{2,1,0:T(8,128)(2,1)} fusion(bf16[24,256,128]{2,1,0:T(8,128)(2,1)S(1)} %bitcast.117, s32[1024]{0:T(1024)S(1)} %pad_clamp_fusion.1), kind=kCustom, calls=%fused_computation.2 | custom fusion | bytes 8388864 | tf_op jit(solution)/shard_map/jit(_take)/gather | solution.py:344
  47.2 4.5 %broadcast_select_fusion = bf16[64,256,128]{2,1,0:T(8,128)(2,1)} fusion(bf16[64,256,128]{2,1,0:T(8,128)(2,1)} %gather_fusion.2, pred[64]{0:T(512)(128)(4,1)S(1)} %get-tuple-element.20), kind=kLoop, calls=%fused_computation.5 | loop fusion | flops 2097152 | bytes 8388672 | tf_op jit(solution)/shard_map/jit(_take)/select_n | solution.py:344
  51.7 7.2 %all-to-all-start = ((bf16[64,256,128]{2,1,0:T(8,128)(2,1)}), bf16[64,256,128]{2,1,0:T(8,128)(2,1)}, u32[]{:S(2)}, u32[]{:S(2)}) async-start(bf16[64,256,128]{2,1,0:T(8,128)(2,1)} %broadcast_select_fusion), calls=%async_computation | async-start | bytes 8388608 | tf_op jit(solution)/shard_map/all_to_all | solution.py:345
  59.5 11.7 %cholesky.74 = f32[128,128]{1,0:T(8,128)S(1)} custom-call(f32[128,128]{1,0:T(8,128)S(1)} %fusion.108), custom_call_target="Cholesky" | custom-call | tf_op jit(solution)/shard_map/jit(cholesky)/cholesky | solution.py:257
  71.2 0.6 compare_reduce_fusion.3
  71.8 0.7 fusion.114
  72.5 9.8 %custom-call.12 = f32[1,128,128]{1,2,0:T(8,128)S(1)} custom-call(f32[1,128,128]{2,1,0:T(8,128)S(1)} %get-tuple-element.24), custom_call_target="InvertDiagBlocksLowerTriangular" | custom-call | tf_op jit(solution)/shard_map/jit(_solve_triangular)/triangular_solve | solution.py:258
  83.3 11.7 %cholesky.85 = f32[128,128]{1,0:T(8,128)S(1)} custom-call(f32[128,128]{1,0:T(8,128)S(1)} %fusion.106), custom_call_target="Cholesky" | custom-call | tf_op jit(solution)/shard_map/jit(cholesky)/cholesky | solution.py:260
  95.1 0.6 compare_reduce_fusion.2
  95.7 0.7 fusion.115
  96.4 19.7 %custom-call.13 = f32[1,128,128]{1,2,0:T(8,128)S(1)} custom-call(f32[1,128,128]{2,1,0:T(8,128)S(1)} %get-tuple-element.22), custom_call_target="InvertDiagBlocksLowerTriangular" | custom-call | tf_op jit(solution)/shard_map/jit(_solve_triangular)/triangular_solve | solution.py:261
  116.5 0.5 fusion.37
  117.0 2.3 gather_fusion.1
  119.9 0.6 fusion.56
  120.5 0.4 fusion.62
  121.3 1.2 convolution_convert_fusion.1
  122.6 31.0 %all-to-all-done = bf16[64,256,128]{2,1,0:T(8,128)(2,1)} async-done(((bf16[64,256,128]{2,1,0:T(8,128)(2,1)}), bf16[64,256,128]{2,1,0:T(8,128)(2,1)}, u32[]{:S(2)}, u32[]{:S(2)}) %all-to-all-start) | async-done | bytes 4194336 | tf_op jit(solution)/shard_map/all_to_all | solution.py:345
  153.6 4.7 %fusion.5 = f32[256,256]{0,1:T(8,128)S(1)} fusion(bf16[64,256,128]{2,1,0:T(8,128)(2,1)} %all-to-all-done, f32[1,256,256]{1,2,0:T(8,128)S(1)} %copy.58), kind=kOutput, calls=%fused_computation.19 | convolution fusion | flops 1073807360 | bytes 4718592 | tf_op jit(solution)/shard_map/nbw,ncw->bc/dot_general | solution.py:354
  158.5 11.7 %cholesky.96 = f32[128,128]{1,0:T(8,128)S(1)} custom-call(f32[128,128]{1,0:T(8,128)S(1)} %fusion.104), custom_call_target="Cholesky" | custom-call | tf_op jit(solution)/shard_map/jit(cholesky)/cholesky | solution.py:257
  170.2 0.6 compare_reduce_fusion.1
  170.9 0.7 select_bitcast_fusion.1
  171.5 9.8 %custom-call.14 = f32[1,128,128]{1,2,0:T(8,128)S(1)} custom-call(f32[1,128,128]{2,1,0:T(8,128)S(1)} %get-tuple-element.18), custom_call_target="InvertDiagBlocksLowerTriangular" | custom-call | tf_op jit(solution)/shard_map/jit(_solve_triangular)/triangular_solve | solution.py:258
  182.4 11.9 %cholesky.107 = f32[128,128]{1,0:T(8,128)S(1)} custom-call(f32[128,128]{1,0:T(8,128)S(1)} %fusion.102), custom_call_target="Cholesky" | custom-call | tf_op jit(solution)/shard_map/jit(cholesky)/cholesky | solution.py:260
  194.3 0.6 compare_reduce_fusion
  194.9 0.7 select_bitcast_fusion
  195.6 9.8 %custom-call.15 = f32[1,128,128]{1,2,0:T(8,128)S(1)} custom-call(f32[1,128,128]{2,1,0:T(8,128)S(1)} %get-tuple-element.16), custom_call_target="InvertDiagBlocksLowerTriangular" | custom-call | tf_op jit(solution)/shard_map/jit(_solve_triangular)/triangular_solve | solution.py:261
  206.3 0.5 fusion.31
  206.8 2.3 gather_fusion.3
  209.2 0.6 fusion.51
  209.7 0.4 fusion.65
  210.3 0.7 maximum_maximum_fusion.a_ref
  211.1 43.4 %shard_map.105 = bf16[32,272,128]{2,1,0:T(8,128)(2,1)} custom-call(bf16[272,128]{1,0:T(8,128)(2,1)} %maximum_maximum_fusion.a_ref), custom_call_target="tpu_custom_call" | custom-call | bytes 4456448 | tf_op jit(solution)/shard_map/pallas_call | solution.py:207
  254.5 3.6 %gather_fusion.4 = bf16[24,272,128]{2,1,0:T(8,128)(2,1)} fusion(bf16[32,272,128]{2,1,0:T(8,128)(2,1)} %shard_map.105, s32[1024]{0:T(1024)S(1)} %pad_clamp_fusion), kind=kCustom, calls=%fused_computation.4 | custom fusion | bytes 3342432 | tf_op jit(solution)/shard_map/jit(_take)/gather | solution.py:356
  258.1 1.7 broadcast_select_fusion.1
  259.8 0.4 fusion.12
  260.2 0.4 fusion.6
  260.6 0.4 fusion.8
  261.0 0.4 fusion.15
  261.4 0.5 add_add_fusion
  261.8 0.8 multiply_add_fusion
  262.7 1.7 convolution_convert_fusion
  (74 shorter events, 5.8 us)
Async XLA Ops:
  0.6 3.4 %copy-start = (bf16[6,256,128]{2,1,0:T(8,128)(2,1)S(1)}, bf16[6,256,128]{2,1,0:T(8,128)(2,1)}, u32[]{:S(2)}) copy-start(bf16[6,256,128]{2,1,0:T(8,128)(2,1)} %param.13) | copy-start | bytes 1179652
  2.3 41.8 %copy-start.1 = (bf16[6,4,256,128]{3,2,1,0:T(8,128)(2,1)S(1)}, bf16[6,4,256,128]{3,2,1,0:T(8,128)(2,1)}, u32[]{:S(2)}) copy-start(bf16[6,4,256,128]{3,2,1,0:T(8,128)(2,1)} %param.12) | copy-start | bytes 4718596
  51.7 7.4 %copy-start.3 = (f32[256,256]{1,0:T(8,128)S(1)}, f32[256,256]{1,0:T(8,128)}, u32[]{:S(2)}) copy-start(f32[256,256]{1,0:T(8,128)} %param.19) | copy-start | bytes 786436
  51.7 101.9 %all-to-all-start = ((bf16[64,256,128]{2,1,0:T(8,128)(2,1)}), bf16[64,256,128]{2,1,0:T(8,128)(2,1)}, u32[]{:S(2)}, u32[]{:S(2)}) async-start(bf16[64,256,128]{2,1,0:T(8,128)(2,1)} %broadcast_select_fusion), calls=%async_computation | async-start | bytes 8388608 | tf_op jit(solution)/shard_map/all_to_all | solution.py:345
  59.3 57.3 %copy-start.5 = (f32[256,256]{1,0:T(8,128)S(1)}, f32[256,256]{1,0:T(8,128)}, u32[]{:S(2)}) copy-start(f32[256,256]{1,0:T(8,128)} %param.20) | copy-start | bytes 786436
  119.4 1.6 copy-start.4
  119.7 1.6 copy-start.2
  158.3 48.0 %copy-start.6 = (f32[1,256,256]{2,1,0:T(8,128)S(1)}, f32[1,256,256]{2,1,0:T(8,128)}, u32[]{:S(2)}) copy-start(f32[1,256,256]{2,1,0:T(8,128)} %param.18) | copy-start | bytes 786436

commit v6 on v5

--- a/solution.py
+++ b/solution.py
@@ -341,7 +341,8 @@
     slots = jnp.arange(devices_sub * capacity, dtype=jnp.int32)
     match = position[None, :] == slots[:, None]
     source = jnp.where(jnp.any(match, axis=1), jnp.argmax(match, axis=1), item_count)
-    outgoing = jnp.take(flat_panels, source, axis=0, mode="fill", fill_value=0)
+    with_zero = jnp.concatenate([flat_panels, jnp.zeros((1, height, breadth), flat_panels.dtype)], axis=0)
+    outgoing = jnp.take(with_zero, source, axis=0, mode="clip")
     incoming = lax.all_to_all(outgoing, "sub", split_axis=0, concat_axis=0, tiled=True)
     root_panel_adjoint = (
         -2.0

time: 268 us -> 266 us (level)
  other arithmetic: 110 us -> 105 us
  local copies, waits for them, and re-layouts: 17 us -> 19.8 us
    select_n x1, other arithmetic: 4.5 us -> 0.01 us  [body(): jnp.where(jnp.any(match, axis=1), jnp.argmax(match, axis=1), item_count)]
where the time goes in v6:
time: 266 us; the launch traced here: 263 us
  other arithmetic  105 us (39%)
  Pallas kernels  81.4 us (31%)
  waiting for transfers between devices  31 us (12%)
  local copies, waits for them, and re-layouts  19.8 us (7%)
  matrix products  16.8 us (6%)
  starting transfers between devices  7.24 us (3%)
    pallas_call x1, Pallas kernels, gather_sub(): pl.pallas_call(_gather_kernel, out_shape=jax.ShapeDtypeStruct((32, rows,...  43.4 us
    pallas_call x1, Pallas kernels, allreduce_root(): pl.pallas_call(_allreduce_kernel, out_shape=jax.ShapeDtypeStruct((512, 12...  38 us
    all_to_all x1, waiting for transfers between devices, body(): lax.all_to_all(outgoing, 'sub', split_axis=0, concat_axis=0, tiled=True)  31 us
    another operation x4, other arithmetic, factor_and_inverse(): i22 = jax.scipy.linalg.solve_triangular(f22, identity, lower=True)  30.9 us
    another operation x6, other arithmetic, factor_and_inverse(): f22 = jnp.linalg.cholesky(schur[h:, h:] - _dot(f21, f21.T))  24.9 us
    another operation x6, other arithmetic, factor_and_inverse(): f11 = jnp.linalg.cholesky(schur[:h, :h])  24.8 us
    another operation x4, other arithmetic, factor_and_inverse(): i11 = jax.scipy.linalg.solve_triangular(f11, identity, lower=True)  20.9 us
    all_to_all x1, starting transfers between devices, body(): lax.all_to_all(outgoing, 'sub', split_axis=0, concat_axis=0, tiled=True)  7.24 us
  transfers between devices with their start and end apart: 1, of which 1 were waited for; matrix products, arithmetic and copies ran while one was open for 24% of the time, Pallas kernels for 0%

profile of v6, /device:TPU:128, one launch (start us, length us, event | category | flops | bytes accessed | tf_op | source)
XLA Modules:
  0.0 262.9 jit_solution(10327998155899420869)
XLA Ops:
  0.6 0.8 copy.56
  2.0 0.7 reshape.183.x_ref
  2.7 0.7 dynamic-slice_bitcast_fusion
  3.4 0.7 gather_fusion
  4.4 0.6 iota_reduce_fusion
  5.1 38.0 %shard_map.104 = f32[512,128]{1,0:T(8,128)} custom-call(f32[512,128]{1,0:T(8,128)} %reshape.183.x_ref), custom_call_target="tpu_custom_call" | custom-call | flops 262144 | bytes 786432 | tf_op jit(solution)/shard_map/pallas_call | solution.py:119
  43.1 1.0 reshape.184
  44.2 1.4 concatenate.63
  45.6 4.4 %gather_fusion.2 = bf16[64,256,128]{2,1,0:T(8,128)(2,1)} fusion(bf16[25,256,128]{2,1,0:T(8,128)(2,1)} %concatenate.63, s32[1024]{0:T(1024)S(1)} %pad_clamp_fusion.1), kind=kCustom, calls=%fused_computation.2 | custom fusion | bytes 8388864 | tf_op jit(solution)/shard_map/jit(_take)/gather | solution.py:345
  50.0 7.2 %all-to-all-start = ((bf16[64,256,128]{2,1,0:T(8,128)(2,1)}), bf16[64,256,128]{2,1,0:T(8,128)(2,1)}, u32[]{:S(2)}, u32[]{:S(2)}) async-start(bf16[64,256,128]{2,1,0:T(8,128)(2,1)} %gather_fusion.2), calls=%async_computation | async-start | bytes 8388608 | tf_op jit(solution)/shard_map/all_to_all | solution.py:346
  57.8 11.7 %cholesky.74 = f32[128,128]{1,0:T(8,128)S(1)} custom-call(f32[128,128]{1,0:T(8,128)S(1)} %fusion.108), custom_call_target="Cholesky" | custom-call | tf_op jit(solution)/shard_map/jit(cholesky)/cholesky | solution.py:257
  69.5 0.6 compare_reduce_fusion.3
  70.1 0.7 fusion.114
  70.8 9.8 %custom-call.12 = f32[1,128,128]{1,2,0:T(8,128)S(1)} custom-call(f32[1,128,128]{2,1,0:T(8,128)S(1)} %get-tuple-element.22), custom_call_target="InvertDiagBlocksLowerTriangular" | custom-call | tf_op jit(solution)/shard_map/jit(_solve_triangular)/triangular_solve | solution.py:258
  81.6 11.7 %cholesky.85 = f32[128,128]{1,0:T(8,128)S(1)} custom-call(f32[128,128]{1,0:T(8,128)S(1)} %fusion.106), custom_call_target="Cholesky" | custom-call | tf_op jit(solution)/shard_map/jit(cholesky)/cholesky | solution.py:260
  93.4 0.6 compare_reduce_fusion.2
  94.0 0.7 fusion.115
  94.7 19.7 %custom-call.13 = f32[1,128,128]{1,2,0:T(8,128)S(1)} custom-call(f32[1,128,128]{2,1,0:T(8,128)S(1)} %get-tuple-element.20), custom_call_target="InvertDiagBlocksLowerTriangular" | custom-call | tf_op jit(solution)/shard_map/jit(_solve_triangular)/triangular_solve | solution.py:261
  114.8 0.5 fusion.37
  115.3 2.3 gather_fusion.1
  118.2 0.6 fusion.56
  118.8 0.4 fusion.62
  119.6 1.2 convolution_convert_fusion.1
  120.9 31.0 %all-to-all-done = bf16[64,256,128]{2,1,0:T(8,128)(2,1)} async-done(((bf16[64,256,128]{2,1,0:T(8,128)(2,1)}), bf16[64,256,128]{2,1,0:T(8,128)(2,1)}, u32[]{:S(2)}, u32[]{:S(2)}) %all-to-all-start) | async-done | bytes 4194336 | tf_op jit(solution)/shard_map/all_to_all | solution.py:346
  151.9 4.7 %fusion.5 = f32[256,256]{0,1:T(8,128)S(1)} fusion(bf16[64,256,128]{2,1,0:T(8,128)(2,1)} %all-to-all-done, f32[1,256,256]{1,2,0:T(8,128)S(1)} %copy.58), kind=kOutput, calls=%fused_computation.18 | convolution fusion | flops 1073807360 | bytes 4718592 | tf_op jit(solution)/shard_map/nbw,ncw->bc/dot_general | solution.py:355
  156.8 11.7 %cholesky.96 = f32[128,128]{1,0:T(8,128)S(1)} custom-call(f32[128,128]{1,0:T(8,128)S(1)} %fusion.104), custom_call_target="Cholesky" | custom-call | tf_op jit(solution)/shard_map/jit(cholesky)/cholesky | solution.py:257
  168.5 0.6 compare_reduce_fusion.1
  169.2 0.7 select_bitcast_fusion.1
  169.8 9.8 %custom-call.14 = f32[1,128,128]{1,2,0:T(8,128)S(1)} custom-call(f32[1,128,128]{2,1,0:T(8,128)S(1)} %get-tuple-element.18), custom_call_target="InvertDiagBlocksLowerTriangular" | custom-call | tf_op jit(solution)/shard_map/jit(_solve_triangular)/triangular_solve | solution.py:258
  180.7 11.9 %cholesky.107 = f32[128,128]{1,0:T(8,128)S(1)} custom-call(f32[128,128]{1,0:T(8,128)S(1)} %fusion.102), custom_call_target="Cholesky" | custom-call | tf_op jit(solution)/shard_map/jit(cholesky)/cholesky | solution.py:260
  192.6 0.6 compare_reduce_fusion
  193.2 0.7 select_bitcast_fusion
  193.9 9.8 %custom-call.15 = f32[1,128,128]{1,2,0:T(8,128)S(1)} custom-call(f32[1,128,128]{2,1,0:T(8,128)S(1)} %get-tuple-element.16), custom_call_target="InvertDiagBlocksLowerTriangular" | custom-call | tf_op jit(solution)/shard_map/jit(_solve_triangular)/triangular_solve | solution.py:261
  204.6 0.5 fusion.31
  205.1 2.3 gather_fusion.3
  207.5 0.6 fusion.51
  208.0 0.4 fusion.65
  208.6 0.7 maximum_maximum_fusion.a_ref
  209.4 43.4 %shard_map.105 = bf16[32,272,128]{2,1,0:T(8,128)(2,1)} custom-call(bf16[272,128]{1,0:T(8,128)(2,1)} %maximum_maximum_fusion.a_ref), custom_call_target="tpu_custom_call" | custom-call | bytes 4456448 | tf_op jit(solution)/shard_map/pallas_call | solution.py:207
  252.8 3.6 %gather_fusion.4 = bf16[24,272,128]{2,1,0:T(8,128)(2,1)} fusion(bf16[32,272,128]{2,1,0:T(8,128)(2,1)} %shard_map.105, s32[1024]{0:T(1024)S(1)} %pad_clamp_fusion), kind=kCustom, calls=%fused_computation.4 | custom fusion | bytes 3342432 | tf_op jit(solution)/shard_map/jit(_take)/gather | solution.py:357
  256.4 1.7 broadcast_select_fusion
  258.1 0.4 fusion.12
  258.5 0.4 fusion.6
  258.9 0.4 fusion.8
  259.3 0.4 fusion.15
  259.7 0.5 add_add_fusion
  260.1 0.8 multiply_add_fusion
  261.0 1.7 convolution_convert_fusion
  (74 shorter events, 5.8 us)
Async XLA Ops:
  0.6 1.0 copy-start
  1.6 42.5 %copy-start.1 = (bf16[6,4,256,128]{3,2,1,0:T(8,128)(2,1)S(1)}, bf16[6,4,256,128]{3,2,1,0:T(8,128)(2,1)}, u32[]{:S(2)}) copy-start(bf16[6,4,256,128]{3,2,1,0:T(8,128)(2,1)} %param.12) | copy-start | bytes 4718596
  50.0 7.4 %copy-start.3 = (f32[256,256]{1,0:T(8,128)S(1)}, f32[256,256]{1,0:T(8,128)}, u32[]{:S(2)}) copy-start(f32[256,256]{1,0:T(8,128)} %param.19) | copy-start | bytes 786436
  50.0 101.9 %all-to-all-start = ((bf16[64,256,128]{2,1,0:T(8,128)(2,1)}), bf16[64,256,128]{2,1,0:T(8,128)(2,1)}, u32[]{:S(2)}, u32[]{:S(2)}) async-start(bf16[64,256,128]{2,1,0:T(8,128)(2,1)} %gather_fusion.2), calls=%async_computation | async-start | bytes 8388608 | tf_op jit(solution)/shard_map/all_to_all | solution.py:346
  57.6 57.3 %copy-start.5 = (f32[256,256]{1,0:T(8,128)S(1)}, f32[256,256]{1,0:T(8,128)}, u32[]{:S(2)}) copy-start(f32[256,256]{1,0:T(8,128)} %param.20) | copy-start | bytes 786436
  117.7 1.6 copy-start.4
  118.0 1.6 copy-start.2
  156.6 47.9 %copy-start.6 = (f32[1,256,256]{2,1,0:T(8,128)S(1)}, f32[1,256,256]{2,1,0:T(8,128)}, u32[]{:S(2)}) copy-start(f32[1,256,256]{2,1,0:T(8,128)} %param.18) | copy-start | bytes 786436

commit v7 on v6

--- a/solution.py
+++ b/solution.py
@@ -7,21 +7,14 @@
 
 MESH = pl.DeviceIdType.MESH
 
-def _allreduce_kernel(
-    x_ref, o_ref, full, a1, a2, a3, rs1, rs2, rs3, rs4, ssem, rsem1, rsem2, rsem3, rsem4, gsem3, gsem2, gsem1
-):
+def _allreduce_kernel(x_ref, o_ref, full, a2, a3, rs2, rs3, rs4, ssem, rsem2, rsem3, rsem4, gsem3, gsem2):
     leaf = lax.axis_index("leaf")
     sub = lax.axis_index("sub")
     c = leaf % 2
     y = leaf // 2
     x = sub // 8
     z = sub % 8
-
-    def core_peer():
-        return (leaf + 1 - 2 * c, sub)
-
-    def x_peer(xx):
-        return (leaf, xx * 8 + z)
+    k = x * 2 + c
 
     def y_peer(yy):
         return (yy * 2 + c, sub)
@@ -29,8 +22,15 @@
     def z_peer(zz):
         return (leaf, x * 8 + zz)
 
-    peers = [core_peer()]
-    peers += [x_peer((x + d) % 4) for d in range(1, 4)]
+    group = []
+    for e in range(2):
+        for d in range(4):
+            if e == 0 and d == 0:
+                continue
+            cc = (c + e) % 2
+            xx = (x + d) % 4
+            group.append((xx * 2 + cc, (y * 2 + cc, xx * 8 + z)))
+    peers = [dev for _, dev in group]
     peers += [y_peer((y + d) % 8) for d in range(1, 8)]
     peers += [z_peer((z + d) % 8) for d in range(1, 8)]
     barrier = pltpu.get_barrier_semaphore()
@@ -52,23 +52,22 @@
             src_ref=dst, dst_ref=dst, send_sem=ssem.at[0], recv_sem=rsem, device_id=dev, device_id_type=MESH
         ).wait_recv()
 
-    mine1 = pl.multiple_of(c * 256, 256)
-    send(x_ref.at[pl.ds(pl.multiple_of((1 - c) * 256, 256), 256)], rs1, rsem1.at[0], core_peer())
-    recv_wait(rs1, rsem1.at[0], core_peer())
-    a1[...] = x_ref[pl.ds(mine1, 256), :] + rs1[...]
-
-    for d in range(1, 4):
-        xx = (x + d) % 4
-        send(a1.at[pl.ds(pl.multiple_of(xx * 64, 64), 64)], rs2.at[x], rsem2.at[x], x_peer(xx))
-    for d in range(1, 4):
-        xx = (x + d) % 4
-        recv_wait(rs2.at[xx], rsem2.at[xx], x_peer(xx))
-    rs2[x] = a1[pl.ds(pl.multiple_of(x * 64, 64), 64), :]
-    a2[...] = rs2[0] + rs2[1] + rs2[2] + rs2[3]
+    def chunk(ref, kk, rows):
+        return ref.at[pl.ds(pl.multiple_of(kk * rows, rows), rows)]
+
+    for kk, dev in group:
+        send(chunk(x_ref, kk, 64), rs2.at[k], rsem2.at[k], dev)
+    for kk, dev in group:
+        recv_wait(rs2.at[kk], rsem2.at[kk], dev)
+    rs2[k] = x_ref[pl.ds(pl.multiple_of(k * 64, 64), 64), :]
+    total2 = rs2[0]
+    for i in range(1, 8):
+        total2 = total2 + rs2[i]
+    a2[...] = total2
 
     for d in range(1, 8):
         yy = (y + d) % 8
-        send(a2.at[pl.ds(pl.multiple_of(yy * 8, 8), 8)], rs3.at[y], rsem3.at[y], y_peer(yy))
+        send(chunk(a2, yy, 8), rs3.at[y], rsem3.at[y], y_peer(yy))
     for d in range(1, 8):
         yy = (y + d) % 8
         recv_wait(rs3.at[yy], rsem3.at[yy], y_peer(yy))
@@ -88,26 +87,21 @@
     total4 = rs4[0]
     for i in range(1, 8):
         total4 = total4 + rs4[i]
-    base2 = c * 256 + x * 64
-    full[pl.ds(pl.multiple_of(base2 + y * 8, 8), 8), :] = total4
+    base = k * 64
+    full[pl.ds(pl.multiple_of(base + y * 8, 8), 8), :] = total4
 
     for d in range(1, 8):
         yy = (y + d) % 8
-        blk = full.at[pl.ds(pl.multiple_of(base2 + y * 8, 8), 8)]
+        blk = full.at[pl.ds(pl.multiple_of(base + y * 8, 8), 8)]
         send(blk, blk, gsem3.at[y], y_peer(yy))
     for d in range(1, 8):
         yy = (y + d) % 8
-        recv_wait(full.at[pl.ds(pl.multiple_of(base2 + yy * 8, 8), 8)], gsem3.at[yy], y_peer(yy))
-    for d in range(1, 4):
-        xx = (x + d) % 4
-        blk = full.at[pl.ds(pl.multiple_of(base2, 64), 64)]
-        send(blk, blk, gsem2.at[x], x_peer(xx))
-    for d in range(1, 4):
-        xx = (x + d) % 4
-        recv_wait(full.at[pl.ds(pl.multiple_of(c * 256 + xx * 64, 64), 64)], gsem2.at[xx], x_peer(xx))
-    blk = full.at[pl.ds(mine1, 256)]
-    send(blk, blk, gsem1.at[0], core_peer())
-    recv_wait(full.at[pl.ds(pl.multiple_of((1 - c) * 256, 256), 256)], gsem1.at[0], core_peer())
+        recv_wait(full.at[pl.ds(pl.multiple_of(base + yy * 8, 8), 8)], gsem3.at[yy], y_peer(yy))
+    own = chunk(full, k, 64)
+    for kk, dev in group:
+        send(own, own, gsem2.at[k], dev)
+    for kk, dev in group:
+        recv_wait(chunk(full, kk, 64), gsem2.at[kk], dev)
     for cp in sends:
         cp.wait_send()
     o_ref[...] = full[...]
@@ -115,7 +109,7 @@
 
 def allreduce_root(gram):
     flat = gram.reshape(512, 128)
-    n_sends = 1 + 3 + 7 + 7 + 7 + 3 + 1
+    n_sends = 7 * 5
     out = pl.pallas_call(
         _allreduce_kernel,
         out_shape=jax.ShapeDtypeStruct((512, 128), jnp.float32),
@@ -123,21 +117,17 @@
         out_specs=pl.BlockSpec(memory_space=pltpu.VMEM),
         scratch_shapes=[
             pltpu.VMEM((512, 128), jnp.float32),
-            pltpu.VMEM((256, 128), jnp.float32),
             pltpu.VMEM((64, 128), jnp.float32),
             pltpu.VMEM((8, 128), jnp.float32),
-            pltpu.VMEM((256, 128), jnp.float32),
-            pltpu.VMEM((4, 64, 128), jnp.float32),
+            pltpu.VMEM((8, 64, 128), jnp.float32),
             pltpu.VMEM((8, 8, 128), jnp.float32),
             pltpu.VMEM((8, 8, 128), jnp.float32),
             pltpu.SemaphoreType.DMA((n_sends,)),
-            pltpu.SemaphoreType.DMA((1,)),
-            pltpu.SemaphoreType.DMA((4,)),
-            pltpu.SemaphoreType.DMA((8,)),
-            pltpu.SemaphoreType.DMA((8,)),
-            pltpu.SemaphoreType.DMA((8,)),
-            pltpu.SemaphoreType.DMA((4,)),
-            pltpu.SemaphoreType.DMA((1,)),
+            pltpu.SemaphoreType.DMA((8,)),
+            pltpu.SemaphoreType.DMA((8,)),
+            pltpu.SemaphoreType.DMA((8,)),
+            pltpu.SemaphoreType.DMA((8,)),
+            pltpu.SemaphoreType.DMA((8,)),
         ],
         compiler_params=pltpu.CompilerParams(collective_id=0, has_side_effects=True),
         cost_estimate=pl.CostEstimate(flops=4 * 65536, bytes_accessed=3 * 262144, transcendentals=0),

time: 266 us -> 265 us (level)
  no operation moved by 1% of the time
where the time goes in v7:
time: 265 us; the launch traced here: 262 us
  other arithmetic  105 us (40%)
  Pallas kernels  79.6 us (30%)
  waiting for transfers between devices  31.6 us (12%)
  local copies, waits for them, and re-layouts  19.8 us (7%)
  matrix products  16.8 us (6%)
  starting transfers between devices  7.63 us (3%)
    pallas_call x1, Pallas kernels, gather_sub(): pl.pallas_call(_gather_kernel, out_shape=jax.ShapeDtypeStruct((32, rows,...  43 us
    pallas_call x1, Pallas kernels, allreduce_root(): pl.pallas_call(_allreduce_kernel, out_shape=jax.ShapeDtypeStruct((512, 12...  36.6 us
    all_to_all x1, waiting for transfers between devices, body(): lax.all_to_all(outgoing, 'sub', split_axis=0, concat_axis=0, tiled=True)  31.6 us
    another operation x4, other arithmetic, factor_and_inverse(): i22 = jax.scipy.linalg.solve_triangular(f22, identity, lower=True)  30.9 us
    another operation x6, other arithmetic, factor_and_inverse(): f22 = jnp.linalg.cholesky(schur[h:, h:] - _dot(f21, f21.T))  24.9 us
    another operation x6, other arithmetic, factor_and_inverse(): f11 = jnp.linalg.cholesky(schur[:h, :h])  24.8 us
    another operation x4, other arithmetic, factor_and_inverse(): i11 = jax.scipy.linalg.solve_triangular(f11, identity, lower=True)  20.9 us
    all_to_all x1, starting transfers between devices, body(): lax.all_to_all(outgoing, 'sub', split_axis=0, concat_axis=0, tiled=True)  7.63 us
  transfers between devices with their start and end apart: 1, of which 1 were waited for; matrix products, arithmetic and copies ran while one was open for 24% of the time, Pallas kernels for 0%

profile of v7, /device:TPU:128, one launch (start us, length us, event | category | flops | bytes accessed | tf_op | source)
XLA Modules:
  0.0 262.1 jit_solution(6632383104717589463)
XLA Ops:
  0.6 0.8 copy.56
  2.0 0.7 reshape.183.x_ref
  2.7 0.7 dynamic-slice_bitcast_fusion
  3.4 0.7 gather_fusion
  4.4 0.6 iota_reduce_fusion
  5.1 36.6 %shard_map.104 = f32[512,128]{1,0:T(8,128)} custom-call(f32[512,128]{1,0:T(8,128)} %reshape.183.x_ref), custom_call_target="tpu_custom_call" | custom-call | flops 262144 | bytes 786432 | tf_op jit(solution)/shard_map/pallas_call | solution.py:113
  41.7 1.0 reshape.184
  42.8 1.4 concatenate.63
  44.2 4.4 %gather_fusion.2 = bf16[64,256,128]{2,1,0:T(8,128)(2,1)} fusion(bf16[25,256,128]{2,1,0:T(8,128)(2,1)} %concatenate.63, s32[1024]{0:T(1024)S(1)} %pad_clamp_fusion.1), kind=kCustom, calls=%fused_computation.2 | custom fusion | bytes 8388864 | tf_op jit(solution)/shard_map/jit(_take)/gather | solution.py:335
  48.6 7.6 %all-to-all-start = ((bf16[64,256,128]{2,1,0:T(8,128)(2,1)}), bf16[64,256,128]{2,1,0:T(8,128)(2,1)}, u32[]{:S(2)}, u32[]{:S(2)}) async-start(bf16[64,256,128]{2,1,0:T(8,128)(2,1)} %gather_fusion.2), calls=%async_computation | async-start | bytes 8388608 | tf_op jit(solution)/shard_map/all_to_all | solution.py:336
  56.7 11.7 %cholesky.74 = f32[128,128]{1,0:T(8,128)S(1)} custom-call(f32[128,128]{1,0:T(8,128)S(1)} %fusion.108), custom_call_target="Cholesky" | custom-call | tf_op jit(solution)/shard_map/jit(cholesky)/cholesky | solution.py:247
  68.5 0.6 compare_reduce_fusion.3
  69.1 0.7 fusion.114
  69.8 9.8 %custom-call.12 = f32[1,128,128]{1,2,0:T(8,128)S(1)} custom-call(f32[1,128,128]{2,1,0:T(8,128)S(1)} %get-tuple-element.22), custom_call_target="InvertDiagBlocksLowerTriangular" | custom-call | tf_op jit(solution)/shard_map/jit(_solve_triangular)/triangular_solve | solution.py:248
  80.6 11.7 %cholesky.85 = f32[128,128]{1,0:T(8,128)S(1)} custom-call(f32[128,128]{1,0:T(8,128)S(1)} %fusion.106), custom_call_target="Cholesky" | custom-call | tf_op jit(solution)/shard_map/jit(cholesky)/cholesky | solution.py:250
  92.4 0.6 compare_reduce_fusion.2
  93.0 0.7 fusion.115
  93.7 19.7 %custom-call.13 = f32[1,128,128]{1,2,0:T(8,128)S(1)} custom-call(f32[1,128,128]{2,1,0:T(8,128)S(1)} %get-tuple-element.20), custom_call_target="InvertDiagBlocksLowerTriangular" | custom-call | tf_op jit(solution)/shard_map/jit(_solve_triangular)/triangular_solve | solution.py:251
  113.8 0.5 fusion.37
  114.3 2.3 gather_fusion.1
  117.2 0.6 fusion.56
  117.8 0.4 fusion.62
  118.6 1.2 convolution_convert_fusion.1
  119.8 31.6 %all-to-all-done = bf16[64,256,128]{2,1,0:T(8,128)(2,1)} async-done(((bf16[64,256,128]{2,1,0:T(8,128)(2,1)}), bf16[64,256,128]{2,1,0:T(8,128)(2,1)}, u32[]{:S(2)}, u32[]{:S(2)}) %all-to-all-start) | async-done | bytes 4194336 | tf_op jit(solution)/shard_map/all_to_all | solution.py:336
  151.5 4.7 %fusion.5 = f32[256,256]{0,1:T(8,128)S(1)} fusion(bf16[64,256,128]{2,1,0:T(8,128)(2,1)} %all-to-all-done, f32[1,256,256]{1,2,0:T(8,128)S(1)} %copy.58), kind=kOutput, calls=%fused_computation.18 | convolution fusion | flops 1073807360 | bytes 4718592 | tf_op jit(solution)/shard_map/nbw,ncw->bc/dot_general | solution.py:345
  156.3 11.7 %cholesky.96 = f32[128,128]{1,0:T(8,128)S(1)} custom-call(f32[128,128]{1,0:T(8,128)S(1)} %fusion.104), custom_call_target="Cholesky" | custom-call | tf_op jit(solution)/shard_map/jit(cholesky)/cholesky | solution.py:247
  168.1 0.6 compare_reduce_fusion.1
  168.7 0.7 select_bitcast_fusion.1
  169.4 9.8 %custom-call.14 = f32[1,128,128]{1,2,0:T(8,128)S(1)} custom-call(f32[1,128,128]{2,1,0:T(8,128)S(1)} %get-tuple-element.18), custom_call_target="InvertDiagBlocksLowerTriangular" | custom-call | tf_op jit(solution)/shard_map/jit(_solve_triangular)/triangular_solve | solution.py:248
  180.2 11.9 %cholesky.107 = f32[128,128]{1,0:T(8,128)S(1)} custom-call(f32[128,128]{1,0:T(8,128)S(1)} %fusion.102), custom_call_target="Cholesky" | custom-call | tf_op jit(solution)/shard_map/jit(cholesky)/cholesky | solution.py:250
  192.2 0.6 compare_reduce_fusion
  192.8 0.7 select_bitcast_fusion
  193.5 9.8 %custom-call.15 = f32[1,128,128]{1,2,0:T(8,128)S(1)} custom-call(f32[1,128,128]{2,1,0:T(8,128)S(1)} %get-tuple-element.16), custom_call_target="InvertDiagBlocksLowerTriangular" | custom-call | tf_op jit(solution)/shard_map/jit(_solve_triangular)/triangular_solve | solution.py:251
  204.2 0.5 fusion.31
  204.7 2.3 gather_fusion.3
  207.0 0.6 fusion.51
  207.6 0.4 fusion.65
  208.2 0.7 maximum_maximum_fusion.a_ref
  208.9 43.0 %shard_map.105 = bf16[32,272,128]{2,1,0:T(8,128)(2,1)} custom-call(bf16[272,128]{1,0:T(8,128)(2,1)} %maximum_maximum_fusion.a_ref), custom_call_target="tpu_custom_call" | custom-call | bytes 4456448 | tf_op jit(solution)/shard_map/pallas_call | solution.py:197
  252.0 3.6 %gather_fusion.4 = bf16[24,272,128]{2,1,0:T(8,128)(2,1)} fusion(bf16[32,272,128]{2,1,0:T(8,128)(2,1)} %shard_map.105, s32[1024]{0:T(1024)S(1)} %pad_clamp_fusion), kind=kCustom, calls=%fused_computation.4 | custom fusion | bytes 3342432 | tf_op jit(solution)/shard_map/jit(_take)/gather | solution.py:347
  255.6 1.7 broadcast_select_fusion
  257.3 0.4 fusion.12
  257.7 0.4 fusion.6
  258.1 0.4 fusion.8
  258.5 0.4 fusion.15
  258.9 0.5 add_add_fusion
  259.4 0.8 multiply_add_fusion
  260.2 1.7 convolution_convert_fusion
  (74 shorter events, 5.9 us)
Async XLA Ops:
  0.6 1.0 copy-start
  1.6 41.1 %copy-start.1 = (bf16[6,4,256,128]{3,2,1,0:T(8,128)(2,1)S(1)}, bf16[6,4,256,128]{3,2,1,0:T(8,128)(2,1)}, u32[]{:S(2)}) copy-start(bf16[6,4,256,128]{3,2,1,0:T(8,128)(2,1)} %param.12) | copy-start | bytes 4718596
  48.6 7.8 %copy-start.3 = (f32[256,256]{1,0:T(8,128)S(1)}, f32[256,256]{1,0:T(8,128)}, u32[]{:S(2)}) copy-start(f32[256,256]{1,0:T(8,128)} %param.19) | copy-start | bytes 786436
  48.6 102.8 %all-to-all-start = ((bf16[64,256,128]{2,1,0:T(8,128)(2,1)}), bf16[64,256,128]{2,1,0:T(8,128)(2,1)}, u32[]{:S(2)}, u32[]{:S(2)}) async-start(bf16[64,256,128]{2,1,0:T(8,128)(2,1)} %gather_fusion.2), calls=%async_computation | async-start | bytes 8388608 | tf_op jit(solution)/shard_map/all_to_all | solution.py:336
  56.5 57.3 %copy-start.5 = (f32[256,256]{1,0:T(8,128)S(1)}, f32[256,256]{1,0:T(8,128)}, u32[]{:S(2)}) copy-start(f32[256,256]{1,0:T(8,128)} %param.20) | copy-start | bytes 786436
  116.7 1.6 copy-start.4
  117.0 1.6 copy-start.2
  156.2 47.9 %copy-start.6 = (f32[1,256,256]{2,1,0:T(8,128)S(1)}, f32[1,256,256]{2,1,0:T(8,128)}, u32[]{:S(2)}) copy-start(f32[1,256,256]{2,1,0:T(8,128)} %param.18) | copy-start | bytes 786436

commit v8 on v6

--- a/solution.py
+++ b/solution.py
@@ -145,7 +145,7 @@
     return out.reshape(256, 256)
 
 
-def _gather_kernel(a_ref, o_ref, gathered, ssem, rsz, rsx, lsem):
+def _gather_kernel(a_ref, pick_ref, o_ref, gathered, ssem, rsz, rsx, lsem):
     leaf = lax.axis_index("leaf")
     sub = lax.axis_index("sub")
     x = sub // 8
@@ -199,15 +199,16 @@
     recv_wait(column(x_far, 4, 4), rsx.at[3], (leaf, right))
     for cp in sends:
         cp.wait_send()
-    o_ref[...] = gathered[...]
-
-
-def gather_sub(block):
+    for i in range(o_ref.shape[0]):
+        o_ref[i] = gathered[pick_ref[i]]
+
+
+def gather_sub(block, pick):
     rows = block.shape[0]
     return pl.pallas_call(
         _gather_kernel,
-        out_shape=jax.ShapeDtypeStruct((32, rows, 128), block.dtype),
-        in_specs=[pl.BlockSpec(memory_space=pltpu.VMEM)],
+        out_shape=jax.ShapeDtypeStruct((pick.shape[0], rows, 128), block.dtype),
+        in_specs=[pl.BlockSpec(memory_space=pltpu.VMEM), pl.BlockSpec(memory_space=pltpu.SMEM)],
         out_specs=pl.BlockSpec(memory_space=pltpu.VMEM),
         scratch_shapes=[
             pltpu.VMEM((32, rows, 128), block.dtype),
@@ -218,7 +219,7 @@
         ],
         compiler_params=pltpu.CompilerParams(collective_id=1, has_side_effects=True),
         cost_estimate=pl.CostEstimate(flops=0, bytes_accessed=2 * 32 * rows * 128 * 2, transcendentals=0),
-    )(block)
+    )(block, pick)
 
 
 def pack_symmetric(a):
@@ -354,7 +355,7 @@
     root_grad, incoming = lax.optimization_barrier((root_grad, incoming))
     gram_sum = jnp.einsum("nbw,ncw->bc", incoming, incoming, preferred_element_type=jnp.float32)
     upper_adjoint = adjoint_block(upper_block[0] - gram_sum, upper_cot[0])
-    chosen = jnp.take(gather_sub(pack_symmetric(upper_adjoint)), target, axis=0)
+    chosen = gather_sub(pack_symmetric(upper_adjoint), target)
     panel_adjoint = (-2.0 * packed_times(chosen, flat_panels)).astype(jnp.bfloat16)
     panel_adjoint = panel_adjoint.reshape(rows_dev, blocks_row, height, breadth)
     panel_grad = jnp.einsum(

time: 266 us -> 262 us (0.985)
  local copies, waits for them, and re-layouts: 19.8 us -> 16.2 us
    gather x1 -> x0, local copies, waits for them, and re-layouts: 3.65 us -> none  [body(): chosen = jnp.take(gather_sub(pack_symmetric(upper_adjoint)), target, axis=0)]
where the time goes in v8:
time: 262 us; the launch traced here: 259 us
  other arithmetic  103 us (39%)
  Pallas kernels  81.2 us (31%)
  waiting for transfers between devices  31.1 us (12%)
  matrix products  18 us (7%)
  local copies, waits for them, and re-layouts  16.2 us (6%)
  starting transfers between devices  7.24 us (3%)
    pallas_call x1, Pallas kernels, gather_sub(): pl.pallas_call(_gather_kernel, out_shape=jax.ShapeDtypeStruct((pick.shape...  43.2 us
    pallas_call x1, Pallas kernels, allreduce_root(): pl.pallas_call(_allreduce_kernel, out_shape=jax.ShapeDtypeStruct((512, 12...  38 us
    all_to_all x1, waiting for transfers between devices, body(): lax.all_to_all(outgoing, 'sub', split_axis=0, concat_axis=0, tiled=True)  31.1 us
    another operation x4, other arithmetic, factor_and_inverse(): i22 = jax.scipy.linalg.solve_triangular(f22, identity, lower=True)  30.9 us
    another operation x6, other arithmetic, factor_and_inverse(): f22 = jnp.linalg.cholesky(schur[h:, h:] - _dot(f21, f21.T))  24.9 us
    another operation x6, other arithmetic, factor_and_inverse(): f11 = jnp.linalg.cholesky(schur[:h, :h])  24.8 us
    another operation x4, other arithmetic, factor_and_inverse(): i11 = jax.scipy.linalg.solve_triangular(f11, identity, lower=True)  20.9 us
    all_to_all x1, starting transfers between devices, body(): lax.all_to_all(outgoing, 'sub', split_axis=0, concat_axis=0, tiled=True)  7.24 us
  transfers between devices with their start and end apart: 1, of which 1 were waited for; matrix products, arithmetic and copies ran while one was open for 24% of the time, Pallas kernels for 0%

profile of v8, /device:TPU:128, one launch (start us, length us, event | category | flops | bytes accessed | tf_op | source)
XLA Modules:
  0.0 258.7 jit_solution(13747096772952929949)
XLA Ops:
  0.6 0.8 copy.66
  1.6 0.3 convolution_bitcast_fusion
  2.0 0.7 reshape.143.x_ref
  2.7 0.7 dynamic-slice_bitcast_fusion
  3.4 0.7 gather_fusion.1
  4.4 0.6 iota_reduce_fusion
  5.1 38.0 %shard_map.104 = f32[512,128]{1,0:T(8,128)} custom-call(f32[512,128]{1,0:T(8,128)} %reshape.143.x_ref), custom_call_target="tpu_custom_call" | custom-call | flops 262144 | bytes 786432 | tf_op jit(solution)/shard_map/pallas_call | solution.py:119
  43.1 1.0 reshape.144
  44.2 1.4 concatenate.63
  45.6 4.4 %gather_fusion.2 = bf16[64,256,128]{2,1,0:T(8,128)(2,1)} fusion(bf16[25,256,128]{2,1,0:T(8,128)(2,1)} %concatenate.63, s32[1024]{0:T(1024)S(1)} %pad_clamp_fusion), kind=kCustom, calls=%fused_computation.2 | custom fusion | bytes 8388864 | tf_op jit(solution)/shard_map/jit(_take)/gather | solution.py:346
  50.0 7.2 %all-to-all-start = ((bf16[64,256,128]{2,1,0:T(8,128)(2,1)}), bf16[64,256,128]{2,1,0:T(8,128)(2,1)}, u32[]{:S(2)}, u32[]{:S(2)}) async-start(bf16[64,256,128]{2,1,0:T(8,128)(2,1)} %gather_fusion.2), calls=%async_computation | async-start | bytes 8388608 | tf_op jit(solution)/shard_map/all_to_all | solution.py:347
  57.8 11.7 %cholesky.74 = f32[128,128]{1,0:T(8,128)S(1)} custom-call(f32[128,128]{1,0:T(8,128)S(1)} %fusion.108), custom_call_target="Cholesky" | custom-call | tf_op jit(solution)/shard_map/jit(cholesky)/cholesky | solution.py:258
  69.5 0.6 compare_reduce_fusion.3
  70.1 0.7 fusion.114
  70.8 9.8 %custom-call.12 = f32[1,128,128]{1,2,0:T(8,128)S(1)} custom-call(f32[1,128,128]{2,1,0:T(8,128)S(1)} %get-tuple-element.20), custom_call_target="InvertDiagBlocksLowerTriangular" | custom-call | tf_op jit(solution)/shard_map/jit(_solve_triangular)/triangular_solve | solution.py:259
  81.2 0.3 convolution_subtract_fusion.1
  81.6 11.7 %cholesky.85 = f32[128,128]{1,0:T(8,128)S(1)} custom-call(f32[128,128]{1,0:T(8,128)S(1)} %fusion.106), custom_call_target="Cholesky" | custom-call | tf_op jit(solution)/shard_map/jit(cholesky)/cholesky | solution.py:261
  93.4 0.6 compare_reduce_fusion.2
  94.0 0.7 fusion.115
  94.7 19.7 %custom-call.13 = f32[1,128,128]{1,2,0:T(8,128)S(1)} custom-call(f32[1,128,128]{2,1,0:T(8,128)S(1)} %get-tuple-element.18), custom_call_target="InvertDiagBlocksLowerTriangular" | custom-call | tf_op jit(solution)/shard_map/jit(_solve_triangular)/triangular_solve | solution.py:262
  114.8 0.5 fusion.37
  115.3 2.3 gather_fusion
  118.2 0.6 fusion.56
  118.8 0.4 fusion.62
  119.6 1.2 convolution_convert_fusion.1
  120.8 31.1 %all-to-all-done = bf16[64,256,128]{2,1,0:T(8,128)(2,1)} async-done(((bf16[64,256,128]{2,1,0:T(8,128)(2,1)}), bf16[64,256,128]{2,1,0:T(8,128)(2,1)}, u32[]{:S(2)}, u32[]{:S(2)}) %all-to-all-start) | async-done | bytes 4194336 | tf_op jit(solution)/shard_map/all_to_all | solution.py:347
  151.9 4.7 %fusion.5 = f32[256,256]{0,1:T(8,128)S(1)} fusion(bf16[64,256,128]{2,1,0:T(8,128)(2,1)} %all-to-all-done, f32[1,256,256]{1,2,0:T(8,128)S(1)} %copy.56), kind=kOutput, calls=%fused_computation.16 | convolution fusion | flops 1073807360 | bytes 4718592 | tf_op jit(solution)/shard_map/nbw,ncw->bc/dot_general | solution.py:356
  156.8 11.7 %cholesky.96 = f32[128,128]{1,0:T(8,128)S(1)} custom-call(f32[128,128]{1,0:T(8,128)S(1)} %fusion.104), custom_call_target="Cholesky" | custom-call | tf_op jit(solution)/shard_map/jit(cholesky)/cholesky | solution.py:258
  168.5 0.6 compare_reduce_fusion.1
  169.2 0.7 select_bitcast_fusion.1
  169.8 9.8 %custom-call.14 = f32[1,128,128]{1,2,0:T(8,128)S(1)} custom-call(f32[1,128,128]{2,1,0:T(8,128)S(1)} %get-tuple-element.16), custom_call_target="InvertDiagBlocksLowerTriangular" | custom-call | tf_op jit(solution)/shard_map/jit(_solve_triangular)/triangular_solve | solution.py:259
  180.7 11.8 %cholesky.107 = f32[128,128]{1,0:T(8,128)S(1)} custom-call(f32[128,128]{1,0:T(8,128)S(1)} %fusion.102), custom_call_target="Cholesky" | custom-call | tf_op jit(solution)/shard_map/jit(cholesky)/cholesky | solution.py:261
  192.5 0.6 compare_reduce_fusion
  193.2 0.7 select_bitcast_fusion
  193.9 9.8 %custom-call.15 = f32[1,128,128]{1,2,0:T(8,128)S(1)} custom-call(f32[1,128,128]{2,1,0:T(8,128)S(1)} %get-tuple-element.14), custom_call_target="InvertDiagBlocksLowerTriangular" | custom-call | tf_op jit(solution)/shard_map/jit(_solve_triangular)/triangular_solve | solution.py:262
  204.6 0.5 fusion.31
  205.1 2.3 gather_fusion.3
  207.4 0.6 fusion.51
  208.0 0.4 fusion.65
  208.6 0.7 maximum_maximum_fusion.a_ref
  209.3 43.2 %shard_map.105 = bf16[24,272,128]{2,1,0:T(8,128)(2,1)} custom-call(bf16[272,128]{1,0:T(8,128)(2,1)} %maximum_maximum_fusion.a_ref, s32[24]{0:T(128)} %copy-done.8), custom_call_target="tpu_custom_call" | custom-call | bytes 4456448 | tf_op jit(solution)/shard_map/pallas_call | solution.py:208
  252.6 1.6 fusion.12
  254.3 0.4 fusion.6
  254.7 0.4 fusion.8
  255.1 0.4 fusion.15
  255.5 0.5 add_add_fusion
  255.9 0.8 multiply_add_fusion
  256.8 1.7 convolution_convert_fusion
  (74 shorter events, 5.3 us)
Async XLA Ops:
  0.6 1.0 copy-start
  1.6 42.5 %copy-start.1 = (bf16[6,4,256,128]{3,2,1,0:T(8,128)(2,1)S(1)}, bf16[6,4,256,128]{3,2,1,0:T(8,128)(2,1)}, u32[]{:S(2)}) copy-start(bf16[6,4,256,128]{3,2,1,0:T(8,128)(2,1)} %param.12) | copy-start | bytes 4718596
  4.1 41.5 %copy-start.8 = (s32[24]{0:T(128)}, s32[24]{0:T(128)S(1)}, u32[]{:S(2)}) copy-start(s32[24]{0:T(128)S(1)} %and_select_fusion.pick_ref) | copy-start | bytes 292
  50.0 7.4 %copy-start.4 = (f32[256,256]{1,0:T(8,128)S(1)}, f32[256,256]{1,0:T(8,128)}, u32[]{:S(2)}) copy-start(f32[256,256]{1,0:T(8,128)} %param.19) | copy-start | bytes 786436
  50.0 101.9 %all-to-all-start = ((bf16[64,256,128]{2,1,0:T(8,128)(2,1)}), bf16[64,256,128]{2,1,0:T(8,128)(2,1)}, u32[]{:S(2)}, u32[]{:S(2)}) async-start(bf16[64,256,128]{2,1,0:T(8,128)(2,1)} %gather_fusion.2), calls=%async_computation | async-start | bytes 8388608 | tf_op jit(solution)/shard_map/all_to_all | solution.py:347
  57.6 57.3 %copy-start.6 = (f32[256,256]{1,0:T(8,128)S(1)}, f32[256,256]{1,0:T(8,128)}, u32[]{:S(2)}) copy-start(f32[256,256]{1,0:T(8,128)} %param.20) | copy-start | bytes 786436
  117.7 1.6 copy-start.5
  118.0 1.6 copy-start.3
  156.6 47.9 %copy-start.7 = (f32[1,256,256]{2,1,0:T(8,128)S(1)}, f32[1,256,256]{2,1,0:T(8,128)}, u32[]{:S(2)}) copy-start(f32[1,256,256]{2,1,0:T(8,128)} %param.18) | copy-start | bytes 786436
  252.6 1.7 copy-start.2

commit v9 on v8

--- a/solution.py
+++ b/solution.py
@@ -254,11 +254,17 @@
 
 def factor_and_inverse(schur):
     h = schur.shape[0] // 2
+    return factor_and_inverse_blocks(schur[:h, :h], schur[h:, :h], schur[h:, h:])
+
+
+def factor_and_inverse_blocks(s11, s21, s22):
+    schur = s11
+    h = s11.shape[0]
     identity = jnp.eye(h, dtype=schur.dtype)
-    f11 = jnp.linalg.cholesky(schur[:h, :h])
+    f11 = jnp.linalg.cholesky(s11)
     i11 = jax.scipy.linalg.solve_triangular(f11, identity, lower=True)
-    f21 = _dot(schur[h:, :h], i11.T)
-    f22 = jnp.linalg.cholesky(schur[h:, h:] - _dot(f21, f21.T))
+    f21 = _dot(s21, i11.T)
+    f22 = jnp.linalg.cholesky(s22 - _dot(f21, f21.T))
     i22 = jax.scipy.linalg.solve_triangular(f22, identity, lower=True)
     i21 = -_dot(_dot(i22, f21), i11)
     zero = jnp.zeros((h, h), schur.dtype)
@@ -297,7 +303,11 @@
 
 
 def adjoint_block(schur, cotangent):
-    factor, inverse = factor_and_inverse(schur)
+    return adjoint_of_factor(factor_and_inverse(schur), cotangent)
+
+
+def adjoint_of_factor(factored, cotangent):
+    factor, inverse = factored
     product = jnp.dot(factor.T, cotangent, precision=lax.Precision.HIGHEST)
     lowered = jnp.tril(product) - 0.5 * jnp.diag(jnp.diag(product))
     adjoint_full = jnp.dot(
@@ -353,8 +363,19 @@
         "sbw,swv->sbv", root_panel_adjoint, low_inverse, preferred_element_type=jnp.float32
     ).astype(jnp.bfloat16)
     root_grad, incoming = lax.optimization_barrier((root_grad, incoming))
-    gram_sum = jnp.einsum("nbw,ncw->bc", incoming, incoming, preferred_element_type=jnp.float32)
-    upper_adjoint = adjoint_block(upper_block[0] - gram_sum, upper_cot[0])
+    half = height // 2
+    top, bottom = incoming[:, :half, :], incoming[:, half:, :]
+
+    def gram(a, b):
+        return jnp.einsum("nbw,ncw->bc", a, b, preferred_element_type=jnp.float32)
+
+    block = upper_block[0]
+    factored = factor_and_inverse_blocks(
+        block[:half, :half] - gram(top, top),
+        block[half:, :half] - gram(bottom, top),
+        block[half:, half:] - gram(bottom, bottom),
+    )
+    upper_adjoint = adjoint_of_factor(factored, upper_cot[0])
     chosen = gather_sub(pack_symmetric(upper_adjoint), target)
     panel_adjoint = (-2.0 * packed_times(chosen, flat_panels)).astype(jnp.bfloat16)
     panel_adjoint = panel_adjoint.reshape(rows_dev, blocks_row, height, breadth)

time: 262 us -> 266 us (1.015)
  matrix products: 18 us -> 22.1 us
    dot_general x7 -> x9, matrix products: 7.63 us -> 11.7 us  [the longest x3 8.81 us: gram(): return jnp.einsum('nbw,ncw->bc', a, b, preferred_element_type=jnp.float32)]
where the time goes in v9:
time: 266 us; the launch traced here: 263 us
  other arithmetic  103 us (39%)
  Pallas kernels  81.3 us (31%)
  waiting for transfers between devices  31.1 us (12%)
  matrix products  22.1 us (8%)
  local copies, waits for them, and re-layouts  16.2 us (6%)
  starting transfers between devices  7.24 us (3%)
    pallas_call x1, Pallas kernels, gather_sub(): pl.pallas_call(_gather_kernel, out_shape=jax.ShapeDtypeStruct((pick.shape...  43.2 us
    pallas_call x1, Pallas kernels, allreduce_root(): pl.pallas_call(_allreduce_kernel, out_shape=jax.ShapeDtypeStruct((512, 12...  38 us
    all_to_all x1, waiting for transfers between devices, body(): lax.all_to_all(outgoing, 'sub', split_axis=0, concat_axis=0, tiled=True)  31.1 us
    another operation x4, other arithmetic, factor_and_inverse_blocks(): i22 = jax.scipy.linalg.solve_triangular(f22, identity, lower=True)  30.9 us
    another operation x6, other arithmetic, factor_and_inverse_blocks(): f22 = jnp.linalg.cholesky(s22 - _dot(f21, f21.T))  24.9 us
    another operation x6, other arithmetic, factor_and_inverse_blocks(): f11 = jnp.linalg.cholesky(s11)  24.8 us
    another operation x4, other arithmetic, factor_and_inverse_blocks(): i11 = jax.scipy.linalg.solve_triangular(f11, identity, lower=True)  20.9 us
    dot_general x3, matrix products, gram(): return jnp.einsum('nbw,ncw->bc', a, b, preferred_element_type=jnp.float32)  8.81 us
  transfers between devices with their start and end apart: 1, of which 1 were waited for; matrix products, arithmetic and copies ran while one was open for 24% of the time, Pallas kernels for 0%

profile of v9, /device:TPU:128, one launch (start us, length us, event | category | flops | bytes accessed | tf_op | source)
XLA Modules:
  0.0 262.8 jit_solution(16984208264567277265)
XLA Ops:
  0.6 0.8 copy.68
  2.0 0.7 reshape.143.x_ref
  2.7 0.7 dynamic-slice_bitcast_fusion
  3.4 0.7 gather_fusion.1
  4.4 0.6 iota_reduce_fusion
  5.1 38.0 %shard_map.104 = f32[512,128]{1,0:T(8,128)} custom-call(f32[512,128]{1,0:T(8,128)} %reshape.143.x_ref), custom_call_target="tpu_custom_call" | custom-call | flops 262144 | bytes 786432 | tf_op jit(solution)/shard_map/pallas_call | solution.py:119
  43.1 1.0 reshape.144
  44.2 1.4 concatenate.63
  45.6 4.4 %gather_fusion.2 = bf16[64,256,128]{2,1,0:T(8,128)(2,1)} fusion(bf16[25,256,128]{2,1,0:T(8,128)(2,1)} %concatenate.63, s32[1024]{0:T(1024)S(1)} %pad_clamp_fusion), kind=kCustom, calls=%fused_computation.2 | custom fusion | bytes 8388864 | tf_op jit(solution)/shard_map/jit(_take)/gather | solution.py:356
  50.0 7.2 %all-to-all-start = ((bf16[64,256,128]{2,1,0:T(8,128)(2,1)}), bf16[64,256,128]{2,1,0:T(8,128)(2,1)}, u32[]{:S(2)}, u32[]{:S(2)}) async-start(bf16[64,256,128]{2,1,0:T(8,128)(2,1)} %gather_fusion.2), calls=%async_computation | async-start | bytes 8388608 | tf_op jit(solution)/shard_map/all_to_all | solution.py:357
  57.8 11.7 %cholesky.74 = f32[128,128]{1,0:T(8,128)S(1)} custom-call(f32[128,128]{1,0:T(8,128)S(1)} %fusion.134), custom_call_target="Cholesky" | custom-call | tf_op jit(solution)/shard_map/jit(cholesky)/cholesky | solution.py:264
  69.5 0.6 compare_reduce_fusion.3
  70.1 0.7 fusion.140
  70.8 9.8 %custom-call.12 = f32[1,128,128]{1,2,0:T(8,128)S(1)} custom-call(f32[1,128,128]{2,1,0:T(8,128)S(1)} %get-tuple-element.20), custom_call_target="InvertDiagBlocksLowerTriangular" | custom-call | tf_op jit(solution)/shard_map/jit(_solve_triangular)/triangular_solve | solution.py:265
  81.6 11.7 %cholesky.85 = f32[128,128]{1,0:T(8,128)S(1)} custom-call(f32[128,128]{1,0:T(8,128)S(1)} %fusion.132), custom_call_target="Cholesky" | custom-call | tf_op jit(solution)/shard_map/jit(cholesky)/cholesky | solution.py:267
  93.4 0.6 compare_reduce_fusion.2
  94.0 0.7 fusion.141
  94.7 19.7 %custom-call.13 = f32[1,128,128]{1,2,0:T(8,128)S(1)} custom-call(f32[1,128,128]{2,1,0:T(8,128)S(1)} %get-tuple-element.18), custom_call_target="InvertDiagBlocksLowerTriangular" | custom-call | tf_op jit(solution)/shard_map/jit(_solve_triangular)/triangular_solve | solution.py:268
  114.8 0.5 fusion.65
  115.3 2.3 gather_fusion
  118.2 0.6 fusion.84
  118.8 0.4 fusion.90
  119.6 1.2 convolution_convert_fusion.1
  120.8 31.1 %all-to-all-done = bf16[64,256,128]{2,1,0:T(8,128)(2,1)} async-done(((bf16[64,256,128]{2,1,0:T(8,128)(2,1)}), bf16[64,256,128]{2,1,0:T(8,128)(2,1)}, u32[]{:S(2)}, u32[]{:S(2)}) %all-to-all-start) | async-done | bytes 4194336 | tf_op jit(solution)/shard_map/all_to_all | solution.py:357
  151.9 2.9 %fusion.31 = f32[128,128]{0,1:T(8,128)S(1)} fusion(bf16[64,256,128]{2,1,0:T(8,128)(2,1)} %all-to-all-done, f32[256,256]{0,1:T(8,128)S(1)} %bitcast.126), kind=kOutput, calls=%fused_computation.31 | convolution fusion | flops 268451840 | bytes 2228224 | tf_op jit(solution)/shard_map/nbw,ncw->bc/dot_general | solution.py:370
  154.8 2.9 %fusion.23 = f32[128,128]{0,1:T(8,128)S(1)} fusion(bf16[64,256,128]{2,1,0:T(8,128)(2,1)} %all-to-all-done, f32[256,256]{0,1:T(8,128)S(1)} %bitcast.127), kind=kOutput, calls=%fused_computation.29 | convolution fusion | flops 268451840 | bytes 4325376 | tf_op jit(solution)/shard_map/nbw,ncw->bc/dot_general | solution.py:370
  157.8 2.9 %fusion.28 = f32[128,128]{0,1:T(8,128)S(1)} fusion(bf16[64,256,128]{2,1,0:T(8,128)(2,1)} %all-to-all-done, f32[256,256]{0,1:T(8,128)S(1)} %bitcast.128), kind=kOutput, calls=%fused_computation.30 | convolution fusion | flops 268451840 | bytes 2228224 | tf_op jit(solution)/shard_map/nbw,ncw->bc/dot_general | solution.py:370
  160.9 11.7 %cholesky.96 = f32[128,128]{1,0:T(8,128)S(1)} custom-call(f32[128,128]{1,0:T(8,128)S(1)} %fusion.130), custom_call_target="Cholesky" | custom-call | tf_op jit(solution)/shard_map/jit(cholesky)/cholesky | solution.py:264
  172.6 0.6 compare_reduce_fusion.1
  173.2 0.7 select_bitcast_fusion.1
  173.9 9.8 %custom-call.14 = f32[1,128,128]{1,2,0:T(8,128)S(1)} custom-call(f32[1,128,128]{2,1,0:T(8,128)S(1)} %get-tuple-element.16), custom_call_target="InvertDiagBlocksLowerTriangular" | custom-call | tf_op jit(solution)/shard_map/jit(_solve_triangular)/triangular_solve | solution.py:265
  184.7 11.8 %cholesky.107 = f32[128,128]{1,0:T(8,128)S(1)} custom-call(f32[128,128]{1,0:T(8,128)S(1)} %fusion.128), custom_call_target="Cholesky" | custom-call | tf_op jit(solution)/shard_map/jit(cholesky)/cholesky | solution.py:267
  196.6 0.6 compare_reduce_fusion
  197.3 0.7 select_bitcast_fusion
  197.9 9.8 %custom-call.15 = f32[1,128,128]{1,2,0:T(8,128)S(1)} custom-call(f32[1,128,128]{2,1,0:T(8,128)S(1)} %get-tuple-element.14), custom_call_target="InvertDiagBlocksLowerTriangular" | custom-call | tf_op jit(solution)/shard_map/jit(_solve_triangular)/triangular_solve | solution.py:268
  208.6 0.5 fusion.59
  209.1 2.3 gather_fusion.3
  211.5 0.6 fusion.79
  212.1 0.4 fusion.93
  212.7 0.7 maximum_maximum_fusion.a_ref
  213.4 43.2 %shard_map.105 = bf16[24,272,128]{2,1,0:T(8,128)(2,1)} custom-call(bf16[272,128]{1,0:T(8,128)(2,1)} %maximum_maximum_fusion.a_ref, s32[24]{0:T(128)} %copy-done.8), custom_call_target="tpu_custom_call" | custom-call | bytes 4456448 | tf_op jit(solution)/shard_map/pallas_call | solution.py:208
  256.7 1.6 fusion.40
  258.4 0.4 fusion.34
  258.8 0.4 fusion.36
  259.2 0.4 fusion.43
  259.6 0.5 add_add_fusion
  260.0 0.8 multiply_add_fusion
  260.8 1.7 convolution_convert_fusion
  (75 shorter events, 5.9 us)
Async XLA Ops:
  0.6 1.0 copy-start
  1.6 42.5 %copy-start.1 = (bf16[6,4,256,128]{3,2,1,0:T(8,128)(2,1)S(1)}, bf16[6,4,256,128]{3,2,1,0:T(8,128)(2,1)}, u32[]{:S(2)}) copy-start(bf16[6,4,256,128]{3,2,1,0:T(8,128)(2,1)} %param.12) | copy-start | bytes 4718596
  4.1 41.5 %copy-start.8 = (s32[24]{0:T(128)}, s32[24]{0:T(128)S(1)}, u32[]{:S(2)}) copy-start(s32[24]{0:T(128)S(1)} %and_select_fusion.pick_ref) | copy-start | bytes 292
  50.0 7.4 %copy-start.4 = (f32[256,256]{1,0:T(8,128)S(1)}, f32[256,256]{1,0:T(8,128)}, u32[]{:S(2)}) copy-start(f32[256,256]{1,0:T(8,128)} %param.19) | copy-start | bytes 786436
  50.0 101.9 %all-to-all-start = ((bf16[64,256,128]{2,1,0:T(8,128)(2,1)}), bf16[64,256,128]{2,1,0:T(8,128)(2,1)}, u32[]{:S(2)}, u32[]{:S(2)}) async-start(bf16[64,256,128]{2,1,0:T(8,128)(2,1)} %gather_fusion.2), calls=%async_computation | async-start | bytes 8388608 | tf_op jit(solution)/shard_map/all_to_all | solution.py:357
  57.6 57.3 %copy-start.6 = (f32[256,256]{1,0:T(8,128)S(1)}, f32[256,256]{1,0:T(8,128)}, u32[]{:S(2)}) copy-start(f32[256,256]{1,0:T(8,128)} %param.20) | copy-start | bytes 786436
  117.7 1.6 copy-start.5
  118.0 1.6 copy-start.3
  160.7 47.9 %copy-start.7 = (f32[1,256,256]{2,1,0:T(8,128)S(1)}, f32[1,256,256]{2,1,0:T(8,128)}, u32[]{:S(2)}) copy-start(f32[1,256,256]{2,1,0:T(8,128)} %param.18) | copy-start | bytes 786436
  256.7 1.7 copy-start.2

commit v10 on v8

--- a/solution.py
+++ b/solution.py
@@ -142,7 +142,7 @@
         compiler_params=pltpu.CompilerParams(collective_id=0, has_side_effects=True),
         cost_estimate=pl.CostEstimate(flops=4 * 65536, bytes_accessed=3 * 262144, transcendentals=0),
     )(flat)
-    return out.reshape(256, 256)
+    return out
 
 
 def _gather_kernel(a_ref, pick_ref, o_ref, gathered, ssem, rsz, rsx, lsem):
@@ -323,8 +323,9 @@
     local_gram = jnp.einsum(
         "sbw,scw->bc", root_panels, root_panels, preferred_element_type=jnp.float32
     )
-    root_total = allreduce_root(local_gram)
-    root_total, panels = lax.optimization_barrier((root_total, panels))
+    root_flat = allreduce_root(local_gram)
+    root_flat, panels = lax.optimization_barrier((root_flat, panels))
+    root_total = root_flat.reshape(local_gram.shape)
     root_adjoint = adjoint_block(root_block - root_total, root_cot)
     rows_dev, blocks_row, height, breadth = panels.shape
     item_count = rows_dev * blocks_row

time: 262 us -> 261 us (level)
  waiting for transfers between devices: 31.1 us -> 40.9 us
  other arithmetic: 103 us -> 93.8 us
    all_to_all x1, waiting for transfers between devices: 31.1 us -> 40.9 us  [body(): lax.all_to_all(outgoing, 'sub', split_axis=0, concat_axis=0, tiled=True)]
    another operation x4, other arithmetic: 30.9 us -> 21.1 us  [factor_and_inverse(): i22 = jax.scipy.linalg.solve_triangular(f22, identity, lower=True)]
  transfers between devices with their start and end apart: 1 -> 1, of which waited for: 1 -> 1; matrix products, arithmetic and copies ran while one was open for 24% -> 21% of each run, Pallas kernels for 0% -> 0%
where the time goes in v10:
time: 261 us; the launch traced here: 258 us
  other arithmetic  93.8 us (36%)
  Pallas kernels  81.3 us (31%)
  waiting for transfers between devices  40.9 us (16%)
  matrix products  18 us (7%)
  local copies, waits for them, and re-layouts  15.3 us (6%)
  starting transfers between devices  7.03 us (3%)
    pallas_call x1, Pallas kernels, gather_sub(): pl.pallas_call(_gather_kernel, out_shape=jax.ShapeDtypeStruct((pick.shape...  43.2 us
    all_to_all x1, waiting for transfers between devices, body(): lax.all_to_all(outgoing, 'sub', split_axis=0, concat_axis=0, tiled=True)  40.9 us
    pallas_call x1, Pallas kernels, allreduce_root(): pl.pallas_call(_allreduce_kernel, out_shape=jax.ShapeDtypeStruct((512, 12...  38 us
    another operation x6, other arithmetic, factor_and_inverse(): f22 = jnp.linalg.cholesky(schur[h:, h:] - _dot(f21, f21.T))  25 us
    another operation x6, other arithmetic, factor_and_inverse(): f11 = jnp.linalg.cholesky(schur[:h, :h])  24.8 us
    another operation x4, other arithmetic, factor_and_inverse(): i22 = jax.scipy.linalg.solve_triangular(f22, identity, lower=True)  21.1 us
    another operation x4, other arithmetic, factor_and_inverse(): i11 = jax.scipy.linalg.solve_triangular(f11, identity, lower=True)  20.9 us
    all_to_all x1, starting transfers between devices, body(): lax.all_to_all(outgoing, 'sub', split_axis=0, concat_axis=0, tiled=True)  7.03 us
  transfers between devices with their start and end apart: 1, of which 1 were waited for; matrix products, arithmetic and copies ran while one was open for 21% of the time, Pallas kernels for 0%

profile of v10, /device:TPU:128, one launch (start us, length us, event | category | flops | bytes accessed | tf_op | source)
XLA Modules:
  0.0 258.1 jit_solution(11296174325617838734)
XLA Ops:
  0.7 0.9 copy.66
  1.7 0.3 convolution_bitcast_fusion
  2.0 0.7 reshape.143.x_ref
  2.8 0.7 dynamic-slice_bitcast_fusion
  3.5 0.7 gather_fusion.1
  4.5 0.6 iota_reduce_fusion
  5.2 38.0 %shard_map.104 = f32[512,128]{1,0:T(8,128)} custom-call(f32[512,128]{1,0:T(8,128)} %reshape.143.x_ref), custom_call_target="tpu_custom_call" | custom-call | flops 262144 | bytes 786432 | tf_op jit(solution)/shard_map/pallas_call | solution.py:119
  43.3 1.4 concatenate.63
  44.7 4.4 %gather_fusion.2 = bf16[64,256,128]{2,1,0:T(8,128)(2,1)} fusion(bf16[25,256,128]{2,1,0:T(8,128)(2,1)} %concatenate.63, s32[1024]{0:T(1024)S(1)} %pad_clamp_fusion), kind=kCustom, calls=%fused_computation.2 | custom fusion | bytes 8388864 | tf_op jit(solution)/shard_map/jit(_take)/gather | solution.py:347
  49.1 7.0 %all-to-all-start = ((bf16[64,256,128]{2,1,0:T(8,128)(2,1)}), bf16[64,256,128]{2,1,0:T(8,128)(2,1)}, u32[]{:S(2)}, u32[]{:S(2)}) async-start(bf16[64,256,128]{2,1,0:T(8,128)(2,1)} %gather_fusion.2), calls=%async_computation | async-start | bytes 8388608 | tf_op jit(solution)/shard_map/all_to_all | solution.py:348
  56.7 11.7 %cholesky.74 = f32[128,128]{1,0:T(8,128)S(1)} custom-call(f32[128,128]{1,0:T(8,128)S(1)} %fusion.108), custom_call_target="Cholesky" | custom-call | tf_op jit(solution)/shard_map/jit(cholesky)/cholesky | solution.py:258
  68.5 0.6 compare_reduce_fusion.3
  69.1 0.7 fusion.114
  69.8 9.8 %custom-call.12 = f32[1,128,128]{1,2,0:T(8,128)S(1)} custom-call(f32[1,128,128]{2,1,0:T(8,128)S(1)} %get-tuple-element.20), custom_call_target="InvertDiagBlocksLowerTriangular" | custom-call | tf_op jit(solution)/shard_map/jit(_solve_triangular)/triangular_solve | solution.py:259
  80.2 0.3 convolution_subtract_fusion.1
  80.6 11.7 %cholesky.85 = f32[128,128]{1,0:T(8,128)S(1)} custom-call(f32[128,128]{1,0:T(8,128)S(1)} %fusion.106), custom_call_target="Cholesky" | custom-call | tf_op jit(solution)/shard_map/jit(cholesky)/cholesky | solution.py:261
  92.3 0.6 compare_reduce_fusion.2
  93.0 0.7 fusion.115
  93.6 10.0 %custom-call.13 = f32[1,128,128]{1,2,0:T(8,128)S(1)} custom-call(f32[1,128,128]{2,1,0:T(8,128)S(1)} %get-tuple-element.18), custom_call_target="InvertDiagBlocksLowerTriangular" | custom-call | tf_op jit(solution)/shard_map/jit(_solve_triangular)/triangular_solve | solution.py:262
  104.0 0.5 fusion.37
  104.6 2.3 gather_fusion
  107.4 0.6 fusion.56
  108.0 0.4 fusion.62
  108.8 1.2 convolution_convert_fusion.1
  110.0 40.9 %all-to-all-done = bf16[64,256,128]{2,1,0:T(8,128)(2,1)} async-done(((bf16[64,256,128]{2,1,0:T(8,128)(2,1)}), bf16[64,256,128]{2,1,0:T(8,128)(2,1)}, u32[]{:S(2)}, u32[]{:S(2)}) %all-to-all-start) | async-done | bytes 4194336 | tf_op jit(solution)/shard_map/all_to_all | solution.py:348
  151.0 4.7 %fusion.5 = f32[256,256]{0,1:T(8,128)S(1)} fusion(bf16[64,256,128]{2,1,0:T(8,128)(2,1)} %all-to-all-done, f32[1,256,256]{1,2,0:T(8,128)S(1)} %copy.56), kind=kOutput, calls=%fused_computation.16 | convolution fusion | flops 1073807360 | bytes 4718592 | tf_op jit(solution)/shard_map/nbw,ncw->bc/dot_general | solution.py:357
  155.8 11.7 %cholesky.96 = f32[128,128]{1,0:T(8,128)S(1)} custom-call(f32[128,128]{1,0:T(8,128)S(1)} %fusion.104), custom_call_target="Cholesky" | custom-call | tf_op jit(solution)/shard_map/jit(cholesky)/cholesky | solution.py:258
  167.6 0.6 compare_reduce_fusion.1
  168.2 0.7 select_bitcast_fusion.1
  168.9 9.8 %custom-call.14 = f32[1,128,128]{1,2,0:T(8,128)S(1)} custom-call(f32[1,128,128]{2,1,0:T(8,128)S(1)} %get-tuple-element.16), custom_call_target="InvertDiagBlocksLowerTriangular" | custom-call | tf_op jit(solution)/shard_map/jit(_solve_triangular)/triangular_solve | solution.py:259
  179.2 0.3 convolution_subtract_fusion
  179.7 11.9 %cholesky.107 = f32[128,128]{1,0:T(8,128)S(1)} custom-call(f32[128,128]{1,0:T(8,128)S(1)} %fusion.102), custom_call_target="Cholesky" | custom-call | tf_op jit(solution)/shard_map/jit(cholesky)/cholesky | solution.py:261
  191.7 0.6 compare_reduce_fusion
  192.3 0.7 select_bitcast_fusion
  193.0 9.8 %custom-call.15 = f32[1,128,128]{1,2,0:T(8,128)S(1)} custom-call(f32[1,128,128]{2,1,0:T(8,128)S(1)} %get-tuple-element.14), custom_call_target="InvertDiagBlocksLowerTriangular" | custom-call | tf_op jit(solution)/shard_map/jit(_solve_triangular)/triangular_solve | solution.py:262
  203.7 0.5 fusion.31
  204.2 2.3 gather_fusion.3
  206.6 0.6 fusion.51
  207.2 0.4 fusion.65
  207.8 0.7 maximum_maximum_fusion.a_ref
  208.5 43.2 %shard_map.105 = bf16[24,272,128]{2,1,0:T(8,128)(2,1)} custom-call(bf16[272,128]{1,0:T(8,128)(2,1)} %maximum_maximum_fusion.a_ref, s32[24]{0:T(128)} %copy-done.9), custom_call_target="tpu_custom_call" | custom-call | bytes 4456448 | tf_op jit(solution)/shard_map/pallas_call | solution.py:208
  251.8 1.6 fusion.12
  253.4 0.4 fusion.6
  253.9 0.4 fusion.8
  254.3 0.4 fusion.15
  254.6 0.5 add_add_fusion
  255.1 0.8 multiply_add_fusion
  255.9 1.7 convolution_convert_fusion
  (76 shorter events, 5.1 us)
Async XLA Ops:
  0.6 1.1 copy-start
  0.6 42.6 %copy-start.1 = (bf16[6,4,256,128]{3,2,1,0:T(8,128)(2,1)S(1)}, bf16[6,4,256,128]{3,2,1,0:T(8,128)(2,1)}, u32[]{:S(2)}) copy-start(bf16[6,4,256,128]{3,2,1,0:T(8,128)(2,1)} %param.12) | copy-start | bytes 4718596
  4.2 40.5 %copy-start.9 = (s32[24]{0:T(128)}, s32[24]{0:T(128)S(1)}, u32[]{:S(2)}) copy-start(s32[24]{0:T(128)S(1)} %and_select_fusion.pick_ref) | copy-start | bytes 292
  49.1 7.0 %copy-start.3 = (f32[512,128]{1,0:T(8,128)S(1)}, f32[512,128]{1,0:T(8,128)}, u32[]{:S(2)}) copy-start(f32[512,128]{1,0:T(8,128)} %shard_map.104) | copy-start | bytes 786436
  49.1 7.3 %copy-start.5 = (f32[256,256]{1,0:T(8,128)S(1)}, f32[256,256]{1,0:T(8,128)}, u32[]{:S(2)}) copy-start(f32[256,256]{1,0:T(8,128)} %param.19) | copy-start | bytes 786436
  49.1 101.8 %all-to-all-start = ((bf16[64,256,128]{2,1,0:T(8,128)(2,1)}), bf16[64,256,128]{2,1,0:T(8,128)(2,1)}, u32[]{:S(2)}, u32[]{:S(2)}) async-start(bf16[64,256,128]{2,1,0:T(8,128)(2,1)} %gather_fusion.2), calls=%async_computation | async-start | bytes 8388608 | tf_op jit(solution)/shard_map/all_to_all | solution.py:348
  56.5 47.5 %copy-start.7 = (f32[256,256]{1,0:T(8,128)S(1)}, f32[256,256]{1,0:T(8,128)}, u32[]{:S(2)}) copy-start(f32[256,256]{1,0:T(8,128)} %param.20) | copy-start | bytes 786436
  106.9 1.6 copy-start.6
  107.2 1.6 copy-start.4
  155.7 48.0 %copy-start.8 = (f32[1,256,256]{2,1,0:T(8,128)S(1)}, f32[1,256,256]{2,1,0:T(8,128)}, u32[]{:S(2)}) copy-start(f32[1,256,256]{2,1,0:T(8,128)} %param.18) | copy-start | bytes 786436
  251.7 1.7 copy-start.2
